TPU v7x, 32 devices: a whole 2x2x4 slice. The times are simulated.
32 devices in a mesh: users: 8 (over z, x), items: 4 (over y, core).
Axes of the slice: x: 2, y: 2, z: 4, core: 2. Of those that a mesh axis runs over, the one named last changes fastest.
Arguments:
- tile_users: int32 [8, 4, 128], P('users', 'items'), may hold values from 0 to 127
- tile_owners: int32 [8, 4, 128, 1], P('users', 'items'), may hold values from 0 to 7; in each aligned block of 128 rows (0 to 127, 128 to 255, ..., all dimensions but the last counted through in order) at most 32 rows name the same one
- tile_blocks: int32 [8, 4, 128], P('users', 'items'), may hold values from 0 to 63
- tile_contexts: int32 [8, 4, 128], P('users', 'items'), may hold values from 0 to 7
- row_users: int32 [8, 4, 128, 128], P('users', 'items'), may hold values from 0 to 15
- row_items: int32 [8, 4, 128, 128], P('users', 'items'), may hold values from 0 to 15
- row_contexts: int32 [8, 4, 128, 128], P('users', 'items'), may hold values from 0 to 127
- tile_values: bfloat16 [8, 4, 128, 128], P('users', 'items'), may hold values from -49152 to 49152
- tile_count: int32 [8, 4], P('users', 'items'), may hold values from 64 to 128, as said below
- item_factors: bfloat16 [8192, 256], P('users'), may hold values from -0.125 to 0.25
- context_factors: bfloat16 [1024, 256], replicated, may hold values from -0.125 to 0.25
- profile: bfloat16 [16384, 2048], P('users', 'items'), may hold values from -192 to 192
- feature_factors: bfloat16 [2048, 256], P('items'), may hold values from -6 to 6
Outputs:
- user_factors: bfloat16 [16384, 256], P('users')
- feature_new: bfloat16 [2048, 256], P('items')
Inputs may be any that keep to these rules, and one draw needn't show every extreme that they name: On one device at most 32 tiles name one index of users in tile_owners, a bound that some block reaches. The live tiles of a device are its first tile_count tiles; some device has all 128 live.
All inputs are finite; a program needn't handle non-finite values.
Results may differ from a plain program's by a relative error of at most 0.00155.
The roundings to bfloat16 on the way count: a program that leaves them out, or rounds other values in their place, can miss the bound.
Values may be sent and summed in bfloat16 or wider, within the bound.
No kernel may reach another device: no remote copies, remote signals or barrier semaphores. Data moves between devices by JAX's collectives and lax.ppermute only.
A program may use at most 64 MiB of HBM per device.

v0:
```python
import jax
import jax.numpy as jnp
from jax import lax
from jax.experimental import pallas as pl
from jax.experimental.pallas import tpu as pltpu
from jax.sharding import PartitionSpec as P

CB = 128
IB = 16
UB = 16
SLAB = 128
RIDGE = 1.0
UNROLL = 32
FLOPS_US = 1000000000
VMEM_GRANT = 16 << 20
PIVOTS = 8
HI = lax.Precision.HIGHEST
VM = pl.BlockSpec(memory_space=pltpu.VMEM)
SM = pl.BlockSpec(memory_space=pltpu.SMEM)
ANY = pl.BlockSpec(memory_space=pl.ANY)
HBM = pl.BlockSpec(memory_space=pltpu.HBM)
F32 = jnp.float32
BF16 = jnp.bfloat16


def gram(matrix):
    return lax.dot_general(
        matrix, matrix, (((0,), (0,)), ((), ())), preferred_element_type=F32
    )


def mm(a, b, dims=(((1,), (0,)), ((), ()))):
    return lax.dot_general(a, b, dims, precision=HI, preferred_element_type=F32)


def solve_pivots(d, r):
    n = len(r)
    if n == 1:
        return [r[0] * (1.0 / d[0][0])]
    h = n // 2
    if n == 2:
        p = 1.0 / d[0][0]
        low = d[0][1] * p
        q = 1.0 / (d[1][1] - d[0][1] * low)
        last = (r[1] - low * r[0]) * q
        return [r[0] * p - low * last, last]
    first = [[d[i][j] if j >= i else None for j in range(h)] for i in range(h)]
    cross = [[d[i][h + j] for j in range(h)] for i in range(h)]
    t = solve_pivots(first, r[:h])
    w = [solve_pivots(first, [cross[i][j] for i in range(h)]) for j in range(h)]
    schur = [
        [
            d[h + i][h + j] - sum(cross[m][i] * w[j][m] for m in range(h)) if j >= i else None
            for j in range(h)
        ]
        for i in range(h)
    ]
    rest = [r[h + i] - sum(cross[m][i] * t[m] for m in range(h)) for i in range(h)]
    q = solve_pivots(schur, rest)
    return [t[m] - sum(w[j][m] * q[j] for j in range(h)) for m in range(h)] + q


def base_inverse(a):
    n = a.shape[0]
    lanes = lax.broadcasted_iota(jnp.int32, (PIVOTS, n), 1)
    lane1 = lax.broadcasted_iota(jnp.int32, (1, n), 1)
    blocks = [a[PIVOTS * i : PIVOTS * (i + 1), :] for i in range(n // PIVOTS)]

    def columns(block, k):
        return [jnp.broadcast_to(block[:, k + j : k + j + 1], (PIVOTS, n)) for j in range(PIVOTS)]

    for v in range(n // PIVOTS):
        k = v * PIVOTS
        pivot = columns(blocks[v], k)
        d = [[pivot[j][i : i + 1, :] for j in range(PIVOTS)] for i in range(PIVOTS)]
        inside = (lane1 >= k) & (lane1 < k + PIVOTS)
        r = [
            jnp.where(inside, (lane1 == k + i).astype(F32), blocks[v][i : i + 1, :])
            for i in range(PIVOTS)
        ]
        rows = [jnp.broadcast_to(x, (PIVOTS, n)) for x in solve_pivots(d, r)]
        inside = (lanes >= k) & (lanes < k + PIVOTS)
        new = []
        for i, block in enumerate(blocks):
            if i == v:
                sub = lax.broadcasted_iota(jnp.int32, (PIVOTS, n), 0)
                x = rows[0]
                for j in range(1, PIVOTS):
                    x = jnp.where(sub == j, rows[j], x)
            else:
                c = columns(block, k)
                x = jnp.where(inside, 0.0, block)
                u = c[0] * rows[0]
                for j in range(1, PIVOTS):
                    u = u + c[j] * rows[j]
                x = x - u
            new.append(x)
        blocks = new
    return jnp.concatenate(blocks, 0)


def inverse_value(a):
    n = a.shape[0]
    if n <= 128:
        return base_inverse(a)
    h = n // 2
    a12 = a[:h, h:]
    i11 = inverse_value(a[:h, :h])
    w = mm(i11, a12)
    i22 = inverse_value(a[h:, h:] - mm(a12, w, (((0,), (0,)), ((), ()))))
    nt = (((1,), (1,)), ((), ()))
    b12 = -mm(w, i22)
    b11 = i11 - mm(b12, w, nt)
    b21 = -mm(i22, w, nt)
    return jnp.concatenate(
        [jnp.concatenate([b11, b12], 1), jnp.concatenate([b21, i22], 1)], 0
    )


def inverse_kernel(ridge, *refs):
    parts, out, full = refs[:-2], refs[-2], refs[-1]
    index = kernel_ids(0)[3]
    for p, part in enumerate(parts):
        rows = part.shape[0]
        full[pl.ds(pl.multiple_of((p ^ index) * rows, rows), rows), :] = part[...]
    a = full[...]
    if ridge:
        same = lax.broadcasted_iota(jnp.int32, a.shape, 0) == lax.broadcasted_iota(
            jnp.int32, a.shape, 1
        )
        a = a + jnp.where(same, RIDGE, 0.0)
    out[...] = inverse_value(a)


def inverse(parts, ridge):
    n = parts[0].shape[1]
    return pl.pallas_call(
        lambda *refs: inverse_kernel(ridge, *refs),
        out_shape=pltpu.VMEM((n, n), F32),
        in_specs=[VM] * len(parts),
        out_specs=VM,
        cost_estimate=cost(11),
    compiler_params=pltpu.CompilerParams(vmem_limit_bytes=VMEM_GRANT),
        scratch_shapes=[pltpu.VMEM((n, n), F32)],
    )(*here(*parts))


def level_sizes(blocks):
    sizes = [1]
    while sum(sizes) < blocks:
        sizes.append(sum(sizes))
    return sizes


def dense_kernel(blocks, profile, features, *refs):
    ids = kernel_ids(0)
    outs, full = refs[:-1], refs[-1]
    f = features[...]
    full[...] = lax.dot_general(f, f, (((0,), (0,)), ((), ())), preferred_element_type=F32)
    rows, small = profile.shape[0] // blocks, full.shape[0] // blocks
    p = 0
    for out in outs:
        for i in range(out.shape[0] // (rows + small)):
            at = p ^ ids[3]
            start = i * (rows + small)
            out[start : start + rows, :] = jnp.dot(
                profile[pl.ds(pl.multiple_of(at * rows, rows), rows), :],
                f,
                preferred_element_type=F32,
            )
            out[start + rows : start + rows + small, :] = full[
                pl.ds(pl.multiple_of(at * small, small), small), :
            ]
            p += 1


def dense_parts(profile, features, blocks):
    n = features.shape[1]
    rows = profile.shape[0] // blocks + n // blocks
    return pl.pallas_call(
        lambda *refs: dense_kernel(blocks, *refs),
        out_shape=[pltpu.VMEM((s * rows, n), F32) for s in level_sizes(blocks)],
        in_specs=[VM, VM],
        cost_estimate=cost(3.7),
        compiler_params=pltpu.CompilerParams(vmem_limit_bytes=VMEM_GRANT),
        out_specs=[VM] * len(level_sizes(blocks)),
        scratch_shapes=[pltpu.VMEM((n, n), F32)],
    )(*here(profile, features))


def solve_kernel(blocks, mine, other, dense, inverse_ref, users_out, *refs):
    outs, full = refs[:-1], refs[-1]
    ids = kernel_ids(0)
    rows = mine.shape[0]
    first = ids[4] == 0
    left = jnp.where(first, mine[...], other[...])
    right = jnp.where(first, other[...], mine[...])
    total = jnp.concatenate([left, right], 1) + dense[:rows, :]
    users = mm(total, inverse_ref[...]).astype(BF16)
    users_out[...] = users
    full[...] = lax.dot_general(
        users, users, (((0,), (0,)), ((), ())), preferred_element_type=F32
    )
    small = full.shape[0] // blocks
    p = 0
    for out in outs:
        for i in range(out.shape[0] // small):
            at = pl.ds(pl.multiple_of((p ^ ids[3]) * small, small), small)
            out[i * small : (i + 1) * small, :] = full[at, :]
            p += 1


def solve_users(mine, other, dense, normal_inverse, blocks):
    n = normal_inverse.shape[0]
    sizes = level_sizes(blocks)
    return pl.pallas_call(
        lambda *refs: solve_kernel(blocks, *refs),
        out_shape=[pltpu.VMEM((mine.shape[0], n), BF16)]
        + [pltpu.VMEM((s * (n // blocks), n), F32) for s in sizes],
        in_specs=[VM, VM, VM, VM],
        cost_estimate=cost(3),
        compiler_params=pltpu.CompilerParams(vmem_limit_bytes=VMEM_GRANT),
        out_specs=[VM] * (1 + len(sizes)),
        scratch_shapes=[pltpu.VMEM((n, n), F32)],
    )(*here(mine, other, dense, normal_inverse))


def kernel_ids(unit):
    top, _, index = item_order()
    me = lax.axis_index("items")
    return lax.axis_index("users"), index * unit, me % top, index, me // top


def here(*arrays):
    return [pltpu.with_memory_space_constraint(x, pltpu.VMEM) for x in arrays]


def cost(microseconds):
    return pl.CostEstimate(
        flops=int(microseconds * FLOPS_US), bytes_accessed=0, transcendentals=0
    )


def prep_kernel(place, blocks_held, count, *refs):
    inputs, (meta, data), scratch, sems = refs[:8], refs[8:10], refs[10:18], refs[18]
    copies = [
        pltpu.make_async_copy(source, target, sems.at[i])
        for i, (source, target) in enumerate(zip(inputs, scratch))
    ]
    for copy in copies:
        copy.start()
    owners, blocks, contexts, users, ru, ri, rc, val = scratch
    ids = kernel_ids(0)
    tiles_here, width = ru.shape
    for copy in copies:
        copy.wait()
    per_slab = SLAB // IB
    block = owners[...] * blocks_held + blocks[...]
    rows = [
        place(block // per_slab, ids),
        contexts[...],
        users[...] * UB,
        block % per_slab * IB,
        jnp.full((1, tiles_here), count[0, 0], jnp.int32),
    ]
    for i, row in enumerate(rows):
        meta[i : i + 1, :] = row
    meta[len(rows) :, :] = jnp.zeros((8 - len(rows), tiles_here), jnp.int32)
    alive = lax.broadcasted_iota(jnp.int32, (tiles_here, width), 0) < count[0, 0]
    data[0] = ru[...].astype(F32).astype(BF16)
    data[1] = ri[...].astype(F32).astype(BF16)
    data[2] = rc[...].astype(F32).astype(BF16)
    data[3] = jnp.where(alive, val[...].astype(F32), 0.0).astype(BF16)


def tiles_kernel(n_tables, unit, meta_hbm, meta_par_hbm, own_hbm, par_hbm, ctx_hbm, *rest):
    tables = rest[:n_tables]
    outs = rest[n_tables:-8]
    table_ref, raw_ref, ctx_ref, data_ref, acc_ref, meta_own, meta_par, sems = rest[-8:]
    total, width = own_hbm.shape[1:]
    copies = [
        pltpu.make_async_copy(own_hbm, raw_ref.at[0], sems.at[0]),
        pltpu.make_async_copy(par_hbm, raw_ref.at[1], sems.at[1]),
        pltpu.make_async_copy(meta_hbm, meta_own, sems.at[2]),
        pltpu.make_async_copy(meta_par_hbm, meta_par, sems.at[3]),
        pltpu.make_async_copy(ctx_hbm, ctx_ref, sems.at[4]),
    ]
    start = 0
    for i, source in enumerate(tables):
        count = source.shape[0]
        copies.append(
            pltpu.make_async_copy(source, table_ref.at[pl.ds(start, count)], sems.at[5 + i])
        )
        start += count
    for copy in copies:
        copy.start()
    acc_ref[...] = jnp.zeros_like(acc_ref)
    copies[0].wait()
    data_ref[:, :total, :] = raw_ref[0].astype(F32)
    copies[1].wait()
    data_ref[:, total:, :] = raw_ref[1].astype(F32)
    big = lax.broadcasted_iota(jnp.int32, (SLAB, width), 0).astype(F32).astype(BF16)
    wide = lax.broadcasted_iota(jnp.int32, (CB, width), 0).astype(F32).astype(BF16)
    small = lax.broadcasted_iota(jnp.int32, (UB, width), 0).astype(F32).astype(BF16)
    one, zero = jnp.ones((), BF16), jnp.zeros((), BF16)
    flip = kernel_ids(unit)[1]
    copies[2].wait()
    copies[3].wait()
    own_groups = (meta_own[4, 0] + UNROLL - 1) // UNROLL
    groups = own_groups + (meta_par[4, 0] + UNROLL - 1) // UNROLL
    for copy in copies[4:]:
        copy.wait()

    def group(g, _):
        is_own = g < own_groups
        tile = jnp.where(is_own, g, g - own_groups) * UNROLL
        first = pl.multiple_of(tile + jnp.where(is_own, 0, total), UNROLL)
        us, its, cs, vs = (data_ref[j, pl.ds(first, UNROLL), :] for j in range(4))

        def scalar(which, t):
            return jnp.where(is_own, meta_own[which, t], meta_par[which, t])

        for j in range(UNROLL):
            t = tile + j

            def row(x, height):
                return jnp.broadcast_to(x.astype(BF16), (height, width))

            items = its[j : j + 1, :] + scalar(3, t).astype(F32)
            pick_item = jnp.where(row(items, SLAB) == big, one, zero)
            pick_context = jnp.where(row(cs[j : j + 1, :], CB) == wide, one, zero)
            weight = jnp.where(row(us[j : j + 1, :], UB) == small, row(vs[j : j + 1, :], UB), zero)
            a = jnp.dot(table_ref[scalar(0, t)], pick_item, preferred_element_type=F32)
            b = jnp.dot(ctx_ref[scalar(1, t)], pick_context, preferred_element_type=F32)
            p = a * b
            hi = p.astype(BF16)
            lo = (p - hi.astype(F32)).astype(BF16)
            r = lax.dot_general(
                jnp.concatenate([weight, weight], 1),
                jnp.concatenate([hi, lo], 1),
                (((1,), (1,)), ((), ())),
                preferred_element_type=F32,
            )
            at = pl.ds(pl.multiple_of(scalar(2, t) ^ flip, UB), UB)
            acc_ref[at, :] += r
        return 0

    lax.fori_loop(0, groups, group, 0)
    start = 0
    for out in outs:
        out[...] = acc_ref[pl.ds(start, out.shape[0]), :]
        start += out.shape[0]


def swap(x, axis, distance):
    size = lax.axis_size(axis)
    return lax.ppermute(x, axis, [(i, i ^ distance) for i in range(size)])


def halves(size):
    steps = []
    while size > 1:
        size //= 2
        steps.append(size)
    return steps


def take_rows(x, start, count):
    return lax.dynamic_slice_in_dim(x, start, count, 0)


def item_order():
    items_size = lax.axis_size("items")
    top = items_size // 2
    order = halves(top) + [top]
    me = lax.axis_index("items")
    index = 0
    for distance in order:
        index = index * 2 + (me // distance) % 2
    return top, order, index


def after(x, earlier):
    return lax.optimization_barrier((x, earlier))[0]


def scatter_levels(levels, order):
    for distance in order:
        came = swap(levels[-1], "items", distance)
        start, kept = 0, []
        for x in levels[:-1]:
            kept.append(x + came[start : start + x.shape[0]])
            start += x.shape[0]
        levels = kept
    return levels


def joined(x, other, bit):
    return jnp.concatenate([jnp.where(bit == 0, x, other), jnp.where(bit == 0, other, x)], 0)


def gather_users(x, steps):
    me = lax.axis_index("users")
    for distance in steps[::-1]:
        x = joined(x, swap(x, "users", distance), (me // distance) % 2)
    return x


def table_layout(item_factors):
    size = lax.axis_size("users")
    top, _, _ = item_order()
    high = lax.axis_index("items") // top
    low = lax.axis_index("items") % top
    rows, width = item_factors.shape
    cols = width // 2
    if size > 16 or rows % (SLAB * top):
        mine = lax.dynamic_slice_in_dim(item_factors, high * cols, cols, 1)
        return mine, None, lambda slab, ids: slab
    count = rows // top
    mine = lax.dynamic_slice(item_factors, (low * count, high * cols), (count, cols))
    piece = mine.reshape(count // SLAB, SLAB, cols).transpose(0, 2, 1)
    steps = halves(size)
    steps = steps[:1] + steps[:0:-1]
    held, part = rows // SLAB, count // SLAB

    def place(slab, ids):
        owner, inner = slab // held, slab % held
        far = owner ^ ids[0]
        position = sum((far // d % 2) * (1 << n) for n, d in enumerate(steps))
        return ((inner // part ^ ids[2]) * size + position) * part + inner % part

    return piece, steps, place


def local(
    tile_users,
    tile_owners,
    tile_blocks,
    tile_contexts,
    row_users,
    row_items,
    row_contexts,
    tile_values,
    tile_count,
    item_factors,
    context_factors,
    profile,
    feature_factors,
):
    top, order, index = item_order()
    items_size = lax.axis_size("items")
    high = lax.axis_index("items") // top
    tile_total = tile_users.shape[2]
    width = row_users.shape[3]
    rank_width = item_factors.shape[1]
    cols = rank_width // 2
    slab_users = profile.shape[0]
    user_rows = slab_users // items_size
    blocks_held = item_factors.shape[0] // IB
    piece, steps, place = table_layout(item_factors)
    shape = (tile_total, width)
    meta, data = pl.pallas_call(
        lambda *refs: prep_kernel(place, blocks_held, *refs),
        out_shape=(
            pltpu.VMEM((8, tile_total), jnp.int32),
            pltpu.VMEM((4,) + shape, BF16),
        ),
        in_specs=[SM] + [HBM] * 8,
        out_specs=(VM, VM),
        cost_estimate=cost(1.7),
        compiler_params=pltpu.CompilerParams(vmem_limit_bytes=VMEM_GRANT),
        scratch_shapes=[
            *[pltpu.VMEM((1, tile_total), jnp.int32)] * 4,
            *[pltpu.VMEM(shape, jnp.int32)] * 3,
            pltpu.VMEM(shape, BF16),
            pltpu.SemaphoreType.DMA((8,)),
        ],
    )(
        tile_count,
        *[
            pltpu.with_memory_space_constraint(x, pltpu.HBM)
            for x in (
                tile_owners.reshape(1, tile_total),
                tile_blocks.reshape(1, tile_total),
                tile_contexts.reshape(1, tile_total),
                tile_users.reshape(1, tile_total),
                row_users.reshape(shape),
                row_items.reshape(shape),
                row_contexts.reshape(shape),
                tile_values.reshape(shape),
            )
        ],
    )

    user_steps = halves(lax.axis_size("users"))[::-1]
    if steps:
        came = swap(after(piece, data), "users", steps[0])
    rank_rows = rank_width // items_size
    item_part = take_rows(gram(after(item_factors, (data, piece))), index * rank_rows, rank_rows)
    item_other = swap(item_part, "users", user_steps[0])
    levels = dense_parts(after(profile, item_part), feature_factors, items_size)
    meta_other = swap(meta, "items", top)
    data_other = swap(data, "items", top)
    if steps:
        tables = [jnp.concatenate([piece, after(came, levels[-1])], 0)]
        tables += [swap(tables[0], "users", d) for d in steps[1:2]]
        early = [swap(tables[0], "users", d) for d in steps[2:3]]
    else:
        full = lax.all_gather(piece, "users", tiled=True)
        tables, early = [full.reshape(-1, SLAB, cols).transpose(0, 2, 1)], []
    levels = scatter_levels(levels, order[:-1])
    dense_other = swap(levels[1], "items", top)
    late = after(context_factors, levels[1])
    contexts = lax.dynamic_slice_in_dim(late, high * cols, cols, 1)
    contexts = contexts.reshape(-1, CB, cols).transpose(0, 2, 1)
    context_part = take_rows(gram(late), index * rank_rows, rank_rows)
    if early:
        tables = tables + early + [swap(tables[1], "users", steps[2])]
    item_part = item_part + item_other
    for distance in user_steps[1:]:
        item_part = item_part + swap(item_part, "users", distance)
    if steps:
        for distance in halves(top)[::-1]:
            tables = tables + [swap(x, "items", distance) for x in tables]
    dense = levels[0] + after(dense_other, item_part)
    diagonal = (
        index * rank_rows + lax.broadcasted_iota(jnp.int32, item_part.shape, 0)
        == lax.broadcasted_iota(jnp.int32, item_part.shape, 1)
    ).astype(F32)
    normal = [item_part * context_part + dense[user_rows:] + RIDGE * diagonal]
    data_other = after(data_other, normal[0])
    normal = normal + [swap(normal[0], "items", top)]

    sizes = [s * user_rows for s in level_sizes(items_size)]
    levels = pl.pallas_call(
        lambda *refs: tiles_kernel(len(tables), user_rows, *refs),
        name="tiles",
        out_shape=[pltpu.VMEM((n, cols), F32) for n in sizes],
        in_specs=[ANY] * (5 + len(tables)),
        cost_estimate=cost(15),
        compiler_params=pltpu.CompilerParams(vmem_limit_bytes=VMEM_GRANT),
        out_specs=[VM] * len(sizes),
        scratch_shapes=[
            pltpu.VMEM((sum(t.shape[0] for t in tables), cols, SLAB), BF16),
            pltpu.VMEM((2,) + data.shape, BF16),
            pltpu.VMEM(contexts.shape, BF16),
            pltpu.VMEM((4, 2 * tile_total, width), F32),
            pltpu.VMEM((slab_users, cols), F32),
            pltpu.SMEM(meta.shape, jnp.int32),
            pltpu.SMEM(meta.shape, jnp.int32),
            pltpu.SemaphoreType.DMA((5 + len(tables),)),
        ],
    )(*here(meta, meta_other, data, data_other, contexts, *tables))
    mine, near = scatter_levels(levels, order[:-1])
    other = swap(near, "items", top)
    normal[1] = after(normal[1], levels[0])
    for distance in order[-2::-1]:
        normal = normal + [swap(x, "items", distance) for x in normal]
    normal[0] = after(normal[0], near)
    normal_inverse = inverse(normal, False)
    users_part, *levels = solve_users(mine, other, dense, normal_inverse, items_size)

    levels = scatter_levels(levels, order[:-1])
    users_other = swap(after(users_part, levels[1]), "items", top)
    (part,) = scatter_levels(levels, order[-1:])
    sums = [part]
    for distance in user_steps:
        part = part + swap(part, "users", distance)
        sums.append(part)
    users_other = after(users_other, sums[1])
    user_factors = joined(users_part, users_other, high)
    for distance in order[-2::-1]:
        bit = (lax.axis_index("items") // distance) % 2
        user_factors = joined(user_factors, swap(user_factors, "items", distance), bit)
    feature_right = lax.dot_general(
        profile,
        user_factors,
        (((0,), (0,)), ((), ())),
        preferred_element_type=F32,
    )
    gathered = [part]
    for distance in order[::-1]:
        gathered = gathered + [swap(x, "items", distance) for x in gathered]
    users_me = lax.axis_index("users")
    for distance in user_steps[:-1]:
        half = feature_right.shape[0] // 2
        bit = (users_me // distance) % 2
        keep = take_rows(feature_right, bit * half, half)
        send = take_rows(feature_right, (1 - bit) * half, half)
        feature_right = keep + swap(send, "users", distance)
    gathered[0] = after(gathered[0], feature_right)
    user_inverse = inverse(gathered, True)
    for distance in user_steps[-1:]:
        feature_right = feature_right + swap(feature_right, "users", distance)
    feature_part = jnp.dot(feature_right, user_inverse, precision=HI).astype(BF16)
    feature_new = gather_users(feature_part, user_steps[:-1])
    return (user_factors, feature_new)


def solution(mesh):
    in_specs = (
        P("users", "items", None),
        P("users", "items", None, None),
        P("users", "items", None),
        P("users", "items", None),
        P("users", "items", None, None),
        P("users", "items", None, None),
        P("users", "items", None, None),
        P("users", "items", None, None),
        P("users", "items"),
        P("users", None),
        P(),
        P("users", "items"),
        P("items", None),
    )
    out_specs = (P("users", None), P("items", None))
    return jax.shard_map(local, mesh=mesh, in_specs=in_specs, out_specs=out_specs, check_vma=False)
```

profile of v0, /device:TPU:0, one launch (start us, length us, event | category | flops | bytes accessed | tf_op | source)
XLA Modules:
  0.0 125.7 jit_solution(293825826375370191)
XLA Ops:
  6.9 3.7 %collective-permute-start.7 = (bf16[4,128,128]{2,1,0:T(8,128)(2,1)S(1)}, bf16[4,128,128]{2,1,0:T(8,128)(2,1)S(1)}, u32[]{:S(2)}, u32[]{:S(2)}) collective-permute-start(bf16[4,128,128]{2,1,0:T(8,128)(2,1)S(1)} %bitcast.26), channel_id=1, source_target_pairs={{0,16},{4,20},{8,24},{12,28},{16,0},{20,4},{24,8},{28,12},{1,17},{... | collective-permute-start | bytes 393224 | tf_op jit(solution)/shard_map/ppermute | solution.py:357
  12.0 5.4 %collective-permute-done.7 = bf16[4,128,128]{2,1,0:T(8,128)(2,1)S(1)} collective-permute-done((bf16[4,128,128]{2,1,0:T(8,128)(2,1)S(1)}, bf16[4,128,128]{2,1,0:T(8,128)(2,1)S(1)}, u32[]{:S(2)}, u32[]{:S(2)}) %collective-permute-start.7) | collective-permute-done | bytes 131104 | tf_op jit(solution)/shard_map/ppermute | solution.py:357
  23.7 3.1 %collective-permute-done.3 = f32[64,256]{1,0:T(8,128)S(1)} collective-permute-done((f32[64,256]{1,0:T(8,128)S(1)}, f32[64,256]{1,0:T(8,128)S(1)}, u32[]{:S(2)}, u32[]{:S(2)}) %collective-permute-start.3) | collective-permute-done | bytes 65568 | tf_op jit(solution)/shard_map/ppermute | solution.py:357
  26.8 2.1 %collective-permute-start.4 = (f32[64,256]{1,0:T(8,128)S(1)}, f32[64,256]{1,0:T(8,128)S(1)}, u32[]{:S(2)}, u32[]{:S(2)}) collective-permute-start(f32[64,256]{1,0:T(8,128)S(1)} %add.118), channel_id=1, source_target_pairs={{0,16},{4,20},{8,24},{12,28},{16,0},{20,4},{24,8},{28,12},{1,17},{... | collective-permute-start | bytes 196616 | tf_op jit(solution)/shard_map/ppermute | solution.py:357
  28.9 2.0 %collective-permute-start.9 = (bf16[8,128,128]{2,1,0:T(8,128)(2,1)S(1)}, bf16[8,128,128]{2,1,0:T(8,128)(2,1)S(1)}, u32[]{:S(2)}, u32[]{:S(2)}) collective-permute-start(bf16[8,128,128]{2,1,0:T(8,128)(2,1)S(1)} %pad_maximum_fusion.2.refs_5_), channel_id=1, source_target_pairs={{0,8},{4,12},{8,0},{12,4},{16,24},{20,28},{24,16},{28,20},{1,9},{5... | collective-permute-start | bytes 786440 | tf_op jit(solution)/shard_map/ppermute | solution.py:357
  34.5 3.3 %collective-permute-done.9.refs_7_ = bf16[8,128,128]{2,1,0:T(8,128)(2,1)S(1)} collective-permute-done((bf16[8,128,128]{2,1,0:T(8,128)(2,1)S(1)}, bf16[8,128,128]{2,1,0:T(8,128)(2,1)S(1)}, u32[]{:S(2)}, u32[]{:S(2)}) %collective-permute-start.9) | collective-permute-done | bytes 262176 | tf_op jit(solution)/shard_map/ppermute | solution.py:357
  37.8 4.4 %collective-permute-done.10.refs_8_ = bf16[8,128,128]{2,1,0:T(8,128)(2,1)S(1)} collective-permute-done((bf16[8,128,128]{2,1,0:T(8,128)(2,1)S(1)}, bf16[8,128,128]{2,1,0:T(8,128)(2,1)S(1)}, u32[]{:S(2)}, u32[]{:S(2)}) %collective-permute-start.10) | collective-permute-done | bytes 262176 | tf_op jit(solution)/shard_map/ppermute | solution.py:357
  44.7 3.0 %collective-permute-done.refs_1_ = s32[8,128]{1,0:T(8,128)S(1)} collective-permute-done((s32[8,128]{1,0:T(8,128)S(1)}, s32[8,128]{1,0:T(8,128)S(1)}, u32[]{:S(2)}, u32[]{:S(2)}) %collective-permute-start) | collective-permute-done | bytes 4128 | tf_op jit(solution)/shard_map/ppermute | solution.py:357
  47.7 12.3 %tiles.1 = (f32[512,128]{1,0:T(8,128)S(1)}, f32[512,128]{1,0:T(8,128)S(1)}, f32[1024,128]{1,0:T(8,128)S(1)}) custom-call(s32[8,128]{1,0:T(8,128)S(1)} %get-tuple-element.26.refs_0_, s32[8,128]{1,0:T(8,128)S(1)} %collective-permute-done.refs_1_, bf16[4,128,128]{2,1,0:T(8,128)(2,1)S(1)} %copy-done.5, bf16[4,128,128]{2,1,0:T(8,128)(2,1)S(1)} %collective-permute-done.1.refs_3_, ...), custom_call_target="tpu_custom_call" | custom-call | flops 15000000512 | tf_op jit(solution)/shard_map/tiles/pallas_call | solution.py:535
  60.9 3.8 %collective-permute-done.17.refs_1_ = f32[64,256]{1,0:T(8,128)S(1)} collective-permute-done((f32[64,256]{1,0:T(8,128)S(1)}, f32[64,256]{1,0:T(8,128)S(1)}, u32[]{:S(2)}, u32[]{:S(2)}) %collective-permute-start.17) | collective-permute-done | bytes 65568 | tf_op jit(solution)/shard_map/ppermute | solution.py:357
  65.9 8.5 %shard_map.142.refs_3_ = f32[256,256]{1,0:T(8,128)S(1)} custom-call(f32[64,256]{1,0:T(8,128)S(1)} %fusion.3.refs_0_, f32[64,256]{1,0:T(8,128)S(1)} %collective-permute-done.17.refs_1_, f32[64,256]{1,0:T(8,128)S(1)} %collective-permute-done.18.refs_2_, f32[64,256]{1,0:T(8,128)S(1)} %collective-permute-done.19.refs_3_), custom_call_target="tpu_custom_call" | custom-call | flops 11000000512 | tf_op jit(solution)/shard_map/pallas_call | solution.py:137
  78.9 2.9 %collective-permute-done.22 = f32[64,256]{1,0:T(8,128)S(1)} collective-permute-done((f32[64,256]{1,0:T(8,128)S(1)}, f32[64,256]{1,0:T(8,128)S(1)}, u32[]{:S(2)}, u32[]{:S(2)}) %collective-permute-start.22) | collective-permute-done | bytes 65568 | tf_op jit(solution)/shard_map/ppermute | solution.py:357
  81.9 4.2 %collective-permute-done.23 = f32[64,256]{1,0:T(8,128)S(1)} collective-permute-done((f32[64,256]{1,0:T(8,128)S(1)}, f32[64,256]{1,0:T(8,128)S(1)}, u32[]{:S(2)}, u32[]{:S(2)}) %collective-permute-start.23) | collective-permute-done | bytes 65568 | tf_op jit(solution)/shard_map/ppermute | solution.py:357
  86.8 1.9 %collective-permute-done.24 = bf16[1024,256]{1,0:T(8,128)(2,1)S(1)} collective-permute-done((bf16[1024,256]{1,0:T(8,128)(2,1)S(1)}, bf16[1024,256]{1,0:T(8,128)(2,1)S(1)}, u32[]{:S(2)}, u32[]{:S(2)}) %collective-permute-start.24) | collective-permute-done | bytes 524320 | tf_op jit(solution)/shard_map/ppermute | solution.py:357
  89.9 2.3 %collective-permute-start.28 = (f32[64,256]{1,0:T(8,128)S(1)}, f32[64,256]{1,0:T(8,128)S(1)}, u32[]{:S(2)}, u32[]{:S(2)}) collective-permute-start(f32[64,256]{1,0:T(8,128)S(1)} %add.132), channel_id=1, source_target_pairs={{0,8},{4,12},{8,0},{12,4},{16,24},{20,28},{24,16},{28,20},{1,9},{5... | collective-permute-start | bytes 196616 | tf_op jit(solution)/shard_map/ppermute | solution.py:357
  92.2 2.2 %collective-permute-done.28 = f32[64,256]{1,0:T(8,128)S(1)} collective-permute-done((f32[64,256]{1,0:T(8,128)S(1)}, f32[64,256]{1,0:T(8,128)S(1)}, u32[]{:S(2)}, u32[]{:S(2)}) %collective-permute-start.28) | collective-permute-done | bytes 65568 | tf_op jit(solution)/shard_map/ppermute | solution.py:357
  94.5 1.8 %collective-permute-start.29 = (f32[64,256]{1,0:T(8,128)S(1)}, f32[64,256]{1,0:T(8,128)S(1)}, u32[]{:S(2)}, u32[]{:S(2)}) collective-permute-start(f32[64,256]{1,0:T(8,128)S(1)} %add.142), channel_id=1, source_target_pairs={{0,16},{4,20},{8,24},{12,28},{16,0},{20,4},{24,8},{28,12},{1,17},{... | collective-permute-start | bytes 196616 | tf_op jit(solution)/shard_map/ppermute | solution.py:357
  96.3 2.0 %collective-permute-done.25 = f32[256,256]{0,1:T(8,128)S(1)} collective-permute-done((f32[256,256]{0,1:T(8,128)S(1)}, f32[256,256]{0,1:T(8,128)S(1)}, u32[]{:S(2)}, u32[]{:S(2)}) %collective-permute-start.25) | collective-permute-done | bytes 262176 | tf_op jit(solution)/shard_map/ppermute | solution.py:357
  98.4 1.8 %collective-permute-start.26 = (f32[128,256]{0,1:T(8,128)S(1)}, f32[128,256]{0,1:T(8,128)S(1)}, u32[]{:S(2)}, u32[]{:S(2)}) collective-permute-start(f32[128,256]{0,1:T(8,128)S(1)} %constant_dynamic-slice_fusion), channel_id=1, source_target_pairs={{0,8},{4,12},{8,0},{12,4},{16,24},{20,28},{24,16},{28,20},{1,9},{5... | collective-permute-start | bytes 393224 | tf_op jit(solution)/shard_map/ppermute | solution.py:357
  101.3 3.2 %collective-permute-done.30.refs_1_ = f32[64,256]{1,0:T(8,128)S(1)} collective-permute-done((f32[64,256]{1,0:T(8,128)S(1)}, f32[64,256]{1,0:T(8,128)S(1)}, u32[]{:S(2)}, u32[]{:S(2)}) %collective-permute-start.30) | collective-permute-done | bytes 65568 | tf_op jit(solution)/shard_map/ppermute | solution.py:357
  106.1 8.7 %shard_map.144 = f32[256,256]{1,0:T(8,128)S(1)} custom-call(f32[64,256]{1,0:T(8,128)S(1)} %add.143.refs_0_, f32[64,256]{1,0:T(8,128)S(1)} %collective-permute-done.30.refs_1_, f32[64,256]{1,0:T(8,128)S(1)} %collective-permute-done.31.refs_2_, f32[64,256]{1,0:T(8,128)S(1)} %collective-permute-done.32.refs_3_), custom_call_target="tpu_custom_call" | custom-call | flops 11000000512 | tf_op jit(solution)/shard_map/pallas_call | solution.py:137
  115.2 2.1 %collective-permute-start.33 = (bf16[128,256]{1,0:T(8,128)(2,1)S(1)}, bf16[128,256]{1,0:T(8,128)(2,1)S(1)}, u32[]{:S(2)}, u32[]{:S(2)}) collective-permute-start(bf16[128,256]{1,0:T(8,128)(2,1)S(1)} %convolution_convert_fusion), channel_id=1, source_target_pairs={{0,8},{4,12},{8,0},{12,4},{16,24},{20,28},{24,16},{28,20},{1,9},{5... | collective-permute-start | bytes 196616 | tf_op jit(solution)/shard_map/ppermute | solution.py:357
  117.3 2.5 %collective-permute-done.33 = bf16[128,256]{1,0:T(8,128)(2,1)S(1)} collective-permute-done((bf16[128,256]{1,0:T(8,128)(2,1)S(1)}, bf16[128,256]{1,0:T(8,128)(2,1)S(1)}, u32[]{:S(2)}, u32[]{:S(2)}) %collective-permute-start.33) | collective-permute-done | bytes 65568 | tf_op jit(solution)/shard_map/ppermute | solution.py:357
  121.4 3.4 %collective-permute-done.34 = bf16[256,256]{1,0:T(8,128)(2,1)S(1)} collective-permute-done((bf16[256,256]{1,0:T(8,128)(2,1)S(1)}, bf16[256,256]{1,0:T(8,128)(2,1)S(1)}, u32[]{:S(2)}, u32[]{:S(2)}) %collective-permute-start.34) | collective-permute-done | bytes 131104 | tf_op jit(solution)/shard_map/ppermute | solution.py:357
  (109 shorter events, 33.2 us)
Async XLA Ops:
  6.3 12.8 %collective-permute-start.5 = (f32[1152,256]{1,0:T(8,128)S(1)}, f32[1152,256]{1,0:T(8,128)S(1)}, u32[]{:S(2)}, u32[]{:S(2)}) collective-permute-start(f32[1152,256]{1,0:T(8,128)S(1)} %get-tuple-element.31), channel_id=1, source_target_pairs={{0,1},{1,0},{2,3},{3,2},{4,5},{5,4},{6,7},{7,6},{8,9},{9,8},{10,11... | collective-permute-start | bytes 3538952 | tf_op jit(solution)/shard_map/ppermute | solution.py:357
  6.9 10.6 %collective-permute-start.7 = (bf16[4,128,128]{2,1,0:T(8,128)(2,1)S(1)}, bf16[4,128,128]{2,1,0:T(8,128)(2,1)S(1)}, u32[]{:S(2)}, u32[]{:S(2)}) collective-permute-start(bf16[4,128,128]{2,1,0:T(8,128)(2,1)S(1)} %bitcast.26), channel_id=1, source_target_pairs={{0,16},{4,20},{8,24},{12,28},{16,0},{20,4},{24,8},{28,12},{1,17},{... | collective-permute-start | bytes 393224 | tf_op jit(solution)/shard_map/ppermute | solution.py:357
  10.5 11.0 %collective-permute-start.2 = (f32[64,256]{1,0:T(8,128)S(1)}, f32[64,256]{1,0:T(8,128)S(1)}, u32[]{:S(2)}, u32[]{:S(2)}) collective-permute-start(f32[64,256]{1,0:T(8,128)S(1)} %constant_dynamic-slice_fusion.2), channel_id=1, source_target_pairs={{0,4},{4,0},{8,12},{12,8},{16,20},{20,16},{24,28},{28,24},{1,5},{5... | collective-permute-start | bytes 196616 | tf_op jit(solution)/shard_map/ppermute | solution.py:357
  17.4 14.7 %collective-permute-start.8 = (bf16[8,128,128]{2,1,0:T(8,128)(2,1)S(1)}, bf16[8,128,128]{2,1,0:T(8,128)(2,1)S(1)}, u32[]{:S(2)}, u32[]{:S(2)}) collective-permute-start(bf16[8,128,128]{2,1,0:T(8,128)(2,1)S(1)} %pad_maximum_fusion.2.refs_5_), channel_id=1, source_target_pairs={{0,4},{4,0},{8,12},{12,8},{16,20},{20,16},{24,28},{28,24},{1,5},{5... | collective-permute-start | bytes 786440 | tf_op jit(solution)/shard_map/ppermute | solution.py:357
  20.0 22.1 %collective-permute-start.6 = (f32[576,256]{1,0:T(8,128)}, f32[576,256]{1,0:T(8,128)}, u32[]{:S(2)}, u32[]{:S(2)}) collective-permute-start(f32[576,256]{1,0:T(8,128)} %slice_add_fusion.1), channel_id=1, source_target_pairs={{0,2},{1,3},{2,0},{3,1},{4,6},{5,7},{6,4},{7,5},{8,10},{9,11},{10,... | collective-permute-start | bytes 1769480 | tf_op jit(solution)/shard_map/ppermute | solution.py:357
  23.2 20.9 %collective-permute-start.1 = (bf16[4,128,128]{2,1,0:T(8,128)(2,1)S(1)}, bf16[4,128,128]{2,1,0:T(8,128)(2,1)S(1)}, u32[]{:S(2)}, u32[]{:S(2)}) collective-permute-start(bf16[4,128,128]{2,1,0:T(8,128)(2,1)S(1)} %copy-done.5), channel_id=1, source_target_pairs={{0,2},{1,3},{2,0},{3,1},{4,6},{5,7},{6,4},{7,5},{8,10},{9,11},{10,... | collective-permute-start | bytes 393224 | tf_op jit(solution)/shard_map/ppermute | solution.py:357
  26.8 5.4 %collective-permute-start.4 = (f32[64,256]{1,0:T(8,128)S(1)}, f32[64,256]{1,0:T(8,128)S(1)}, u32[]{:S(2)}, u32[]{:S(2)}) collective-permute-start(f32[64,256]{1,0:T(8,128)S(1)} %add.118), channel_id=1, source_target_pairs={{0,16},{4,20},{8,24},{12,28},{16,0},{20,4},{24,8},{28,12},{1,17},{... | collective-permute-start | bytes 196616 | tf_op jit(solution)/shard_map/ppermute | solution.py:357
  28.9 8.9 %collective-permute-start.9 = (bf16[8,128,128]{2,1,0:T(8,128)(2,1)S(1)}, bf16[8,128,128]{2,1,0:T(8,128)(2,1)S(1)}, u32[]{:S(2)}, u32[]{:S(2)}) collective-permute-start(bf16[8,128,128]{2,1,0:T(8,128)(2,1)S(1)} %pad_maximum_fusion.2.refs_5_), channel_id=1, source_target_pairs={{0,8},{4,12},{8,0},{12,4},{16,24},{20,28},{24,16},{28,20},{1,9},{5... | collective-permute-start | bytes 786440 | tf_op jit(solution)/shard_map/ppermute | solution.py:357
  32.1 15.6 %collective-permute-start.11 = (bf16[8,128,128]{2,1,0:T(8,128)(2,1)S(1)}, bf16[8,128,128]{2,1,0:T(8,128)(2,1)S(1)}, u32[]{:S(2)}, u32[]{:S(2)}) collective-permute-start(bf16[8,128,128]{2,1,0:T(8,128)(2,1)S(1)} %pad_maximum_fusion.2.refs_5_), channel_id=1, source_target_pairs={{0,1},{1,0},{2,3},{3,2},{4,5},{5,4},{6,7},{7,6},{8,9},{9,8},{10,11... | collective-permute-start | bytes 786440 | tf_op jit(solution)/shard_map/ppermute | solution.py:357
  32.1 10.0 %collective-permute-start.10 = (bf16[8,128,128]{2,1,0:T(8,128)(2,1)S(1)}, bf16[8,128,128]{2,1,0:T(8,128)(2,1)S(1)}, u32[]{:S(2)}, u32[]{:S(2)}) collective-permute-start(bf16[8,128,128]{2,1,0:T(8,128)(2,1)S(1)} %collective-permute-done.8.refs_6_), channel_id=1, source_target_pairs={{0,8},{4,12},{8,0},{12,4},{16,24},{20,28},{24,16},{28,20},{1,9},{5... | collective-permute-start | bytes 786440 | tf_op jit(solution)/shard_map/ppermute | solution.py:357
  37.7 10.0 %collective-permute-start.12 = (bf16[8,128,128]{2,1,0:T(8,128)(2,1)S(1)}, bf16[8,128,128]{2,1,0:T(8,128)(2,1)S(1)}, u32[]{:S(2)}, u32[]{:S(2)}) collective-permute-start(bf16[8,128,128]{2,1,0:T(8,128)(2,1)S(1)} %collective-permute-done.8.refs_6_), channel_id=1, source_target_pairs={{0,1},{1,0},{2,3},{3,2},{4,5},{5,4},{6,7},{7,6},{8,9},{9,8},{10,11... | collective-permute-start | bytes 786440 | tf_op jit(solution)/shard_map/ppermute | solution.py:357
  42.1 5.6 %collective-permute-start.13 = (bf16[8,128,128]{2,1,0:T(8,128)(2,1)S(1)}, bf16[8,128,128]{2,1,0:T(8,128)(2,1)S(1)}, u32[]{:S(2)}, u32[]{:S(2)}) collective-permute-start(bf16[8,128,128]{2,1,0:T(8,128)(2,1)S(1)} %collective-permute-done.9.refs_7_), channel_id=1, source_target_pairs={{0,1},{1,0},{2,3},{3,2},{4,5},{5,4},{6,7},{7,6},{8,9},{9,8},{10,11... | collective-permute-start | bytes 786440 | tf_op jit(solution)/shard_map/ppermute | solution.py:357
  42.2 5.6 %collective-permute-start.14 = (bf16[8,128,128]{2,1,0:T(8,128)(2,1)S(1)}, bf16[8,128,128]{2,1,0:T(8,128)(2,1)S(1)}, u32[]{:S(2)}, u32[]{:S(2)}) collective-permute-start(bf16[8,128,128]{2,1,0:T(8,128)(2,1)S(1)} %collective-permute-done.10.refs_8_), channel_id=1, source_target_pairs={{0,1},{1,0},{2,3},{3,2},{4,5},{5,4},{6,7},{7,6},{8,9},{9,8},{10,11... | collective-permute-start | bytes 786440 | tf_op jit(solution)/shard_map/ppermute | solution.py:357
  60.1 4.6 %collective-permute-start.15 = (f32[1024,128]{1,0:T(8,128)S(1)}, f32[1024,128]{1,0:T(8,128)S(1)}, u32[]{:S(2)}, u32[]{:S(2)}) collective-permute-start(f32[1024,128]{1,0:T(8,128)S(1)} %get-tuple-element.39), channel_id=1, source_target_pairs={{0,1},{1,0},{2,3},{3,2},{4,5},{5,4},{6,7},{7,6},{8,9},{9,8},{10,11... | collective-permute-start | bytes 1572872 | tf_op jit(solution)/shard_map/ppermute | solution.py:357
  60.7 4.6 %collective-permute-start.18 = (f32[64,256]{1,0:T(8,128)S(1)}, f32[64,256]{1,0:T(8,128)S(1)}, u32[]{:S(2)}, u32[]{:S(2)}) collective-permute-start(f32[64,256]{1,0:T(8,128)S(1)} %fusion.3.refs_0_), channel_id=1, source_target_pairs={{0,1},{1,0},{2,3},{3,2},{4,5},{5,4},{6,7},{7,6},{8,9},{9,8},{10,11... | collective-permute-start | bytes 196616 | tf_op jit(solution)/shard_map/ppermute | solution.py:357
  64.7 9.7 %collective-permute-start.16 = (f32[512,128]{1,0:T(8,128)S(1)}, f32[512,128]{1,0:T(8,128)S(1)}, u32[]{:S(2)}, u32[]{:S(2)}) collective-permute-start(f32[512,128]{1,0:T(8,128)S(1)} %get-tuple-element.54), channel_id=1, source_target_pairs={{0,2},{1,3},{2,0},{3,1},{4,6},{5,7},{6,4},{7,5},{8,10},{9,11},{10,... | collective-permute-start | bytes 786440 | tf_op jit(solution)/shard_map/ppermute | solution.py:357
  76.8 5.0 %collective-permute-start.22 = (f32[64,256]{1,0:T(8,128)S(1)}, f32[64,256]{1,0:T(8,128)S(1)}, u32[]{:S(2)}, u32[]{:S(2)}) collective-permute-start(f32[64,256]{1,0:T(8,128)S(1)} %slice_add_fusion.5), channel_id=1, source_target_pairs={{0,2},{1,3},{2,0},{3,1},{4,6},{5,7},{6,4},{7,5},{8,10},{9,11},{10,... | collective-permute-start | bytes 196616 | tf_op jit(solution)/shard_map/ppermute | solution.py:357
  77.8 8.9 %collective-permute-start.21 = (bf16[512,256]{1,0:T(8,128)(2,1)S(1)}, bf16[512,256]{1,0:T(8,128)(2,1)S(1)}, u32[]{:S(2)}, u32[]{:S(2)}) collective-permute-start(bf16[512,256]{1,0:T(8,128)(2,1)S(1)} %get-tuple-element.46), channel_id=1, source_target_pairs={{0,2},{1,3},{2,0},{3,1},{4,6},{5,7},{6,4},{7,5},{8,10},{9,11},{10,... | collective-permute-start | bytes 786440 | tf_op jit(solution)/shard_map/ppermute | solution.py:357
  89.9 8.3 %collective-permute-start.25 = (f32[256,256]{0,1:T(8,128)S(1)}, f32[256,256]{0,1:T(8,128)S(1)}, u32[]{:S(2)}, u32[]{:S(2)}) collective-permute-start(f32[256,256]{0,1:T(8,128)S(1)} %dynamic-slice_bitcast_fusion), channel_id=1, source_target_pairs={{0,4},{4,0},{8,12},{12,8},{16,20},{20,16},{24,28},{28,24},{1,5},{5... | collective-permute-start | bytes 786440 | tf_op jit(solution)/shard_map/ppermute | solution.py:357
  94.5 5.7 %collective-permute-start.29 = (f32[64,256]{1,0:T(8,128)S(1)}, f32[64,256]{1,0:T(8,128)S(1)}, u32[]{:S(2)}, u32[]{:S(2)}) collective-permute-start(f32[64,256]{1,0:T(8,128)S(1)} %add.142), channel_id=1, source_target_pairs={{0,16},{4,20},{8,24},{12,28},{16,0},{20,4},{24,8},{28,12},{1,17},{... | collective-permute-start | bytes 196616 | tf_op jit(solution)/shard_map/ppermute | solution.py:357
  98.4 6.2 %collective-permute-start.26 = (f32[128,256]{0,1:T(8,128)S(1)}, f32[128,256]{0,1:T(8,128)S(1)}, u32[]{:S(2)}, u32[]{:S(2)}) collective-permute-start(f32[128,256]{0,1:T(8,128)S(1)} %constant_dynamic-slice_fusion), channel_id=1, source_target_pairs={{0,8},{4,12},{8,0},{12,4},{16,24},{20,28},{24,16},{28,20},{1,9},{5... | collective-permute-start | bytes 393224 | tf_op jit(solution)/shard_map/ppermute | solution.py:357
  101.3 4.8 %collective-permute-start.31 = (f32[64,256]{1,0:T(8,128)S(1)}, f32[64,256]{1,0:T(8,128)S(1)}, u32[]{:S(2)}, u32[]{:S(2)}) collective-permute-start(f32[64,256]{1,0:T(8,128)S(1)} %add.143.refs_0_), channel_id=1, source_target_pairs={{0,1},{1,0},{2,3},{3,2},{4,5},{5,4},{6,7},{7,6},{8,9},{9,8},{10,11... | collective-permute-start | bytes 196616 | tf_op jit(solution)/shard_map/ppermute | solution.py:357
  104.5 10.3 %collective-permute-start.27 = (f32[128,256]{0,1:T(8,128)S(1)}, f32[128,256]{0,1:T(8,128)S(1)}, u32[]{:S(2)}, u32[]{:S(2)}) collective-permute-start(f32[128,256]{0,1:T(8,128)S(1)} %dynamic-slice_add_fusion), channel_id=1, source_target_pairs={{0,16},{4,20},{8,24},{12,28},{16,0},{20,4},{24,8},{28,12},{1,17},{... | collective-permute-start | bytes 393224 | tf_op jit(solution)/shard_map/ppermute | solution.py:357
  119.8 5.1 %collective-permute-start.34 = (bf16[256,256]{1,0:T(8,128)(2,1)S(1)}, bf16[256,256]{1,0:T(8,128)(2,1)S(1)}, u32[]{:S(2)}, u32[]{:S(2)}) collective-permute-start(bf16[256,256]{1,0:T(8,128)(2,1)S(1)} %pad_maximum_fusion.4), channel_id=1, source_target_pairs={{0,4},{4,0},{8,12},{12,8},{16,20},{20,16},{24,28},{28,24},{1,5},{5... | collective-permute-start | bytes 393224 | tf_op jit(solution)/shard_map/ppermute | solution.py:357
  (22 other events, 113.3 us)
where the time goes:
time: 126 us
  waiting for transfers between devices  48.9 us (39%)
  starting transfers between devices  33.1 us (26%)
  Pallas kernels  32.5 us (26%)
  other arithmetic  4.6 us (4%)
  local copies, waits for them, and re-layouts  2.93 us (2%)
  matrix products  1.79 us (1%)
  between operations  1.77 us (1%)
    ppermute x35, waiting for transfers between devices, swap(): return lax.ppermute(x, axis, [(i, i ^ distance) for i in range(size)])  48.9 us
    ppermute x35, starting transfers between devices, swap(): return lax.ppermute(x, axis, [(i, i ^ distance) for i in range(size)])  33.1 us
    pallas_call x2, Pallas kernels, inverse(): pl.pallas_call(lambda *refs: inverse_kernel(ridge, *refs), out_shape=pltp...  17.2 us
    pallas_call x1, Pallas kernels, local(): pl.pallas_call(lambda *refs: tiles_kernel(len(tables), user_rows, *refs),...  12.3 us
  transfers between devices with their start and end apart: 35, of which 18 were waited for; matrix products, arithmetic and copies ran while one was open for 3% of the time, Pallas kernels for 14%

commit v1 on v0

--- a/solution.py
+++ b/solution.py
@@ -10,7 +10,7 @@
 UB = 16
 SLAB = 128
 RIDGE = 1.0
-UNROLL = 32
+UNROLL = 64
 FLOPS_US = 1000000000
 VMEM_GRANT = 16 << 20
 PIVOTS = 8
@@ -111,9 +111,8 @@
     nt = (((1,), (1,)), ((), ()))
     b12 = -mm(w, i22)
     b11 = i11 - mm(b12, w, nt)
-    b21 = -mm(i22, w, nt)
     return jnp.concatenate(
-        [jnp.concatenate([b11, b12], 1), jnp.concatenate([b21, i22], 1)], 0
+        [jnp.concatenate([b11, b12], 1), jnp.concatenate([b12.T, i22], 1)], 0
     )
 
 
@@ -496,13 +495,13 @@
     if steps:
         came = swap(after(piece, data), "users", steps[0])
     rank_rows = rank_width // items_size
-    item_part = take_rows(gram(after(item_factors, (data, piece))), index * rank_rows, rank_rows)
+    levels = dense_parts(after(profile, (data, piece)), feature_factors, items_size)
+    item_part = take_rows(gram(after(item_factors, levels[-1])), index * rank_rows, rank_rows)
     item_other = swap(item_part, "users", user_steps[0])
-    levels = dense_parts(after(profile, item_part), feature_factors, items_size)
     meta_other = swap(meta, "items", top)
     data_other = swap(data, "items", top)
     if steps:
-        tables = [jnp.concatenate([piece, after(came, levels[-1])], 0)]
+        tables = [jnp.concatenate([piece, after(came, item_part)], 0)]
         tables += [swap(tables[0], "users", d) for d in steps[1:2]]
         early = [swap(tables[0], "users", d) for d in steps[2:3]]
     else:
@@ -516,7 +515,7 @@
     context_part = take_rows(gram(late), index * rank_rows, rank_rows)
     if early:
         tables = tables + early + [swap(tables[1], "users", steps[2])]
-    item_part = item_part + item_other
+    item_part = item_part + after(item_other, levels[1])
     for distance in user_steps[1:]:
         item_part = item_part + swap(item_part, "users", distance)
     if steps:
@@ -561,7 +560,7 @@
     users_part, *levels = solve_users(mine, other, dense, normal_inverse, items_size)
 
     levels = scatter_levels(levels, order[:-1])
-    users_other = swap(after(users_part, levels[1]), "items", top)
+    users_other = swap(users_part, "items", top)
     (part,) = scatter_levels(levels, order[-1:])
     sums = [part]
     for distance in user_steps:

time: 126 us -> 127 us (level)
  waiting for transfers between devices: 48.9 us -> 47.2 us
  other arithmetic: 4.6 us -> 6.28 us
    ppermute x35, waiting for transfers between devices: 48.9 us -> 47.2 us  [swap(): return lax.ppermute(x, axis, [(i, i ^ distance) for i in range(size)])]
  transfers between devices with their start and end apart: 35 -> 35, of which waited for: 18 -> 18; matrix products, arithmetic and copies ran while one was open for 3% -> 5% of each run, Pallas kernels for 14% -> 14%
where the time goes in v1:
time: 127 us; the launch traced here: 126 us
  waiting for transfers between devices  47.2 us (37%)
  starting transfers between devices  34.2 us (27%)
  Pallas kernels  31.6 us (25%)
  other arithmetic  6.28 us (5%)
  local copies, waits for them, and re-layouts  2.69 us (2%)
  matrix products  2.49 us (2%)
  between operations  1.77 us (1%)
    ppermute x35, waiting for transfers between devices, swap(): return lax.ppermute(x, axis, [(i, i ^ distance) for i in range(size)])  47.2 us
    ppermute x35, starting transfers between devices, swap(): return lax.ppermute(x, axis, [(i, i ^ distance) for i in range(size)])  34.2 us
    pallas_call x2, Pallas kernels, inverse(): pl.pallas_call(lambda *refs: inverse_kernel(ridge, *refs), out_shape=pltp...  17.2 us
    pallas_call x1, Pallas kernels, local(): pl.pallas_call(lambda *refs: tiles_kernel(len(tables), user_rows, *refs),...  11.5 us
  transfers between devices with their start and end apart: 35, of which 18 were waited for; matrix products, arithmetic and copies ran while one was open for 5% of the time, Pallas kernels for 14%

profile of v1, /device:TPU:0, one launch (start us, length us, event | category | flops | bytes accessed | tf_op | source)
XLA Modules:
  0.0 126.3 jit_solution(12536749577716668781)
XLA Ops:
  5.6 3.7 %collective-permute-start.7 = (bf16[4,128,128]{2,1,0:T(8,128)(2,1)S(1)}, bf16[4,128,128]{2,1,0:T(8,128)(2,1)S(1)}, u32[]{:S(2)}, u32[]{:S(2)}) collective-permute-start(bf16[4,128,128]{2,1,0:T(8,128)(2,1)S(1)} %bitcast.26), channel_id=1, source_target_pairs={{0,16},{4,20},{8,24},{12,28},{16,0},{20,4},{24,8},{28,12},{1,17},{... | collective-permute-start | bytes 393224 | tf_op jit(solution)/shard_map/ppermute | solution.py:356
  10.3 5.8 %collective-permute-done.7 = bf16[4,128,128]{2,1,0:T(8,128)(2,1)S(1)} collective-permute-done((bf16[4,128,128]{2,1,0:T(8,128)(2,1)S(1)}, bf16[4,128,128]{2,1,0:T(8,128)(2,1)S(1)}, u32[]{:S(2)}, u32[]{:S(2)}) %collective-permute-start.7) | collective-permute-done | bytes 131104 | tf_op jit(solution)/shard_map/ppermute | solution.py:356
  16.2 1.6 %collective-permute-start.8 = (bf16[8,128,128]{2,1,0:T(8,128)(2,1)S(1)}, bf16[8,128,128]{2,1,0:T(8,128)(2,1)S(1)}, u32[]{:S(2)}, u32[]{:S(2)}) collective-permute-start(bf16[8,128,128]{2,1,0:T(8,128)(2,1)S(1)} %pad_maximum_fusion.2.refs_5_), channel_id=1, source_target_pairs={{0,4},{4,0},{8,12},{12,8},{16,20},{20,16},{24,28},{28,24},{1,5},{5... | collective-permute-start | bytes 786440 | tf_op jit(solution)/shard_map/ppermute | solution.py:356
  20.5 4.5 %collective-permute-done.8.refs_6_ = bf16[8,128,128]{2,1,0:T(8,128)(2,1)S(1)} collective-permute-done((bf16[8,128,128]{2,1,0:T(8,128)(2,1)S(1)}, bf16[8,128,128]{2,1,0:T(8,128)(2,1)S(1)}, u32[]{:S(2)}, u32[]{:S(2)}) %collective-permute-start.8) | collective-permute-done | bytes 262176 | tf_op jit(solution)/shard_map/ppermute | solution.py:356
  31.5 2.4 %collective-permute-done.4 = f32[64,256]{1,0:T(8,128)S(1)} collective-permute-done((f32[64,256]{1,0:T(8,128)S(1)}, f32[64,256]{1,0:T(8,128)S(1)}, u32[]{:S(2)}, u32[]{:S(2)}) %collective-permute-start.4) | collective-permute-done | bytes 65568 | tf_op jit(solution)/shard_map/ppermute | solution.py:356
  33.9 3.4 %collective-permute-start.5 = (f32[64,256]{1,0:T(8,128)S(1)}, f32[64,256]{1,0:T(8,128)}, u32[]{:S(2)}, u32[]{:S(2)}) collective-permute-start(f32[64,256]{1,0:T(8,128)S(1)} %add.119), channel_id=1, source_target_pairs={{0,16},{4,20},{8,24},{12,28},{16,0},{20,4},{24,8},{28,12},{1,17},{... | collective-permute-start | bytes 196616 | tf_op jit(solution)/shard_map/ppermute | solution.py:356
  37.5 2.8 %collective-permute-done.5 = f32[64,256]{1,0:T(8,128)} collective-permute-done((f32[64,256]{1,0:T(8,128)S(1)}, f32[64,256]{1,0:T(8,128)}, u32[]{:S(2)}, u32[]{:S(2)}) %collective-permute-start.5) | collective-permute-done | bytes 65568 | tf_op jit(solution)/shard_map/ppermute | solution.py:356
  44.5 2.7 %collective-permute-done.refs_1_ = s32[8,128]{1,0:T(8,128)S(1)} collective-permute-done((s32[8,128]{1,0:T(8,128)S(1)}, s32[8,128]{1,0:T(8,128)S(1)}, u32[]{:S(2)}, u32[]{:S(2)}) %collective-permute-start) | collective-permute-done | bytes 4128 | tf_op jit(solution)/shard_map/ppermute | solution.py:356
  47.2 11.5 %tiles.1 = (f32[512,128]{1,0:T(8,128)S(1)}, f32[512,128]{1,0:T(8,128)S(1)}, f32[1024,128]{1,0:T(8,128)S(1)}) custom-call(s32[8,128]{1,0:T(8,128)S(1)} %get-tuple-element.26.refs_0_, s32[8,128]{1,0:T(8,128)S(1)} %collective-permute-done.refs_1_, bf16[4,128,128]{2,1,0:T(8,128)(2,1)S(1)} %get-tuple-element.27.refs_2_, ...), custom_call_target="tpu_custom_call" | custom-call | flops 15000000512 | tf_op jit(solution)/shard_map/tiles/pallas_call | solution.py:534
  59.3 4.0 %collective-permute-done.17.refs_1_ = f32[64,256]{1,0:T(8,128)S(1)} collective-permute-done((f32[64,256]{1,0:T(8,128)S(1)}, f32[64,256]{1,0:T(8,128)S(1)}, u32[]{:S(2)}, u32[]{:S(2)}) %collective-permute-start.17) | collective-permute-done | bytes 65568 | tf_op jit(solution)/shard_map/ppermute | solution.py:356
  64.5 8.5 %shard_map.142.refs_3_ = f32[256,256]{1,0:T(8,128)S(1)} custom-call(f32[64,256]{1,0:T(8,128)S(1)} %fusion.3.refs_0_, f32[64,256]{1,0:T(8,128)S(1)} %collective-permute-done.17.refs_1_, f32[64,256]{1,0:T(8,128)S(1)} %collective-permute-done.18.refs_2_, f32[64,256]{1,0:T(8,128)S(1)} %collective-permute-done.19.refs_3_), custom_call_target="tpu_custom_call" | custom-call | flops 11000000512 | tf_op jit(solution)/shard_map/pallas_call | solution.py:136
  77.5 2.9 %collective-permute-done.22 = f32[64,256]{1,0:T(8,128)S(1)} collective-permute-done((f32[64,256]{1,0:T(8,128)S(1)}, f32[64,256]{1,0:T(8,128)S(1)}, u32[]{:S(2)}, u32[]{:S(2)}) %collective-permute-start.22) | collective-permute-done | bytes 65568 | tf_op jit(solution)/shard_map/ppermute | solution.py:356
  80.7 4.1 %collective-permute-done.23 = f32[64,256]{1,0:T(8,128)S(1)} collective-permute-done((f32[64,256]{1,0:T(8,128)S(1)}, f32[64,256]{1,0:T(8,128)S(1)}, u32[]{:S(2)}, u32[]{:S(2)}) %collective-permute-start.23) | collective-permute-done | bytes 65568 | tf_op jit(solution)/shard_map/ppermute | solution.py:356
  85.4 1.9 %collective-permute-done.24 = bf16[1024,256]{1,0:T(8,128)(2,1)S(1)} collective-permute-done((bf16[1024,256]{1,0:T(8,128)(2,1)S(1)}, bf16[1024,256]{1,0:T(8,128)(2,1)S(1)}, u32[]{:S(2)}, u32[]{:S(2)}) %collective-permute-start.24) | collective-permute-done | bytes 524320 | tf_op jit(solution)/shard_map/ppermute | solution.py:356
  88.7 1.9 %collective-permute-start.28 = (f32[64,256]{1,0:T(8,128)S(1)}, f32[64,256]{1,0:T(8,128)S(1)}, u32[]{:S(2)}, u32[]{:S(2)}) collective-permute-start(f32[64,256]{1,0:T(8,128)S(1)} %add.132), channel_id=1, source_target_pairs={{0,8},{4,12},{8,0},{12,4},{16,24},{20,28},{24,16},{28,20},{1,9},{5... | collective-permute-start | bytes 196616 | tf_op jit(solution)/shard_map/ppermute | solution.py:356
  90.6 2.4 %collective-permute-done.28 = f32[64,256]{1,0:T(8,128)S(1)} collective-permute-done((f32[64,256]{1,0:T(8,128)S(1)}, f32[64,256]{1,0:T(8,128)S(1)}, u32[]{:S(2)}, u32[]{:S(2)}) %collective-permute-start.28) | collective-permute-done | bytes 65568 | tf_op jit(solution)/shard_map/ppermute | solution.py:356
  93.0 3.7 %collective-permute-start.29 = (f32[64,256]{1,0:T(8,128)S(1)}, f32[64,256]{1,0:T(8,128)S(1)}, u32[]{:S(2)}, u32[]{:S(2)}) collective-permute-start(f32[64,256]{1,0:T(8,128)S(1)} %add.142), channel_id=1, source_target_pairs={{0,16},{4,20},{8,24},{12,28},{16,0},{20,4},{24,8},{28,12},{1,17},{... | collective-permute-start | bytes 196616 | tf_op jit(solution)/shard_map/ppermute | solution.py:356
  96.9 1.6 %collective-permute-start.26 = (f32[128,256]{0,1:T(8,128)S(1)}, f32[128,256]{0,1:T(8,128)S(1)}, u32[]{:S(2)}, u32[]{:S(2)}) collective-permute-start(f32[128,256]{0,1:T(8,128)S(1)} %constant_dynamic-slice_fusion), channel_id=1, source_target_pairs={{0,8},{4,12},{8,0},{12,4},{16,24},{20,28},{24,16},{28,20},{1,9},{5... | collective-permute-start | bytes 393224 | tf_op jit(solution)/shard_map/ppermute | solution.py:356
  100.3 3.2 %collective-permute-done.30.refs_1_ = f32[64,256]{1,0:T(8,128)S(1)} collective-permute-done((f32[64,256]{1,0:T(8,128)S(1)}, f32[64,256]{1,0:T(8,128)S(1)}, u32[]{:S(2)}, u32[]{:S(2)}) %collective-permute-start.30) | collective-permute-done | bytes 65568 | tf_op jit(solution)/shard_map/ppermute | solution.py:356
  103.5 3.4 %collective-permute-start.27 = (f32[128,256]{0,1:T(8,128)S(1)}, f32[128,256]{0,1:T(8,128)S(1)}, u32[]{:S(2)}, u32[]{:S(2)}) collective-permute-start(f32[128,256]{0,1:T(8,128)S(1)} %dynamic-slice_add_fusion), channel_id=1, source_target_pairs={{0,16},{4,20},{8,24},{12,28},{16,0},{20,4},{24,8},{28,12},{1,17},{... | collective-permute-start | bytes 393224 | tf_op jit(solution)/shard_map/ppermute | solution.py:356
  107.0 8.7 %shard_map.144 = f32[256,256]{1,0:T(8,128)S(1)} custom-call(f32[64,256]{1,0:T(8,128)S(1)} %add.143.refs_0_, f32[64,256]{1,0:T(8,128)S(1)} %collective-permute-done.30.refs_1_, f32[64,256]{1,0:T(8,128)S(1)} %collective-permute-done.31.refs_2_, f32[64,256]{1,0:T(8,128)S(1)} %collective-permute-done.32.refs_3_), custom_call_target="tpu_custom_call" | custom-call | flops 11000000512 | tf_op jit(solution)/shard_map/pallas_call | solution.py:136
  116.1 1.8 %collective-permute-start.33 = (bf16[128,256]{1,0:T(8,128)(2,1)S(1)}, bf16[128,256]{1,0:T(8,128)(2,1)S(1)}, u32[]{:S(2)}, u32[]{:S(2)}) collective-permute-start(bf16[128,256]{1,0:T(8,128)(2,1)S(1)} %convolution_convert_fusion), channel_id=1, source_target_pairs={{0,8},{4,12},{8,0},{12,4},{16,24},{20,28},{24,16},{28,20},{1,9},{5... | collective-permute-start | bytes 196616 | tf_op jit(solution)/shard_map/ppermute | solution.py:356
  117.9 2.6 %collective-permute-done.33 = bf16[128,256]{1,0:T(8,128)(2,1)S(1)} collective-permute-done((bf16[128,256]{1,0:T(8,128)(2,1)S(1)}, bf16[128,256]{1,0:T(8,128)(2,1)S(1)}, u32[]{:S(2)}, u32[]{:S(2)}) %collective-permute-start.33) | collective-permute-done | bytes 65568 | tf_op jit(solution)/shard_map/ppermute | solution.py:356
  120.9 4.6 %collective-permute-done.34 = bf16[256,256]{1,0:T(8,128)(2,1)S(1)} collective-permute-done((bf16[256,256]{1,0:T(8,128)(2,1)S(1)}, bf16[256,256]{1,0:T(8,128)(2,1)S(1)}, u32[]{:S(2)}, u32[]{:S(2)}) %collective-permute-start.34) | collective-permute-done | bytes 131104 | tf_op jit(solution)/shard_map/ppermute | solution.py:356
  (101 shorter events, 30.9 us)
Async XLA Ops:
  5.0 20.9 %collective-permute-start.3 = (f32[1152,256]{1,0:T(8,128)S(1)}, f32[1152,256]{1,0:T(8,128)}, u32[]{:S(2)}, u32[]{:S(2)}) collective-permute-start(f32[1152,256]{1,0:T(8,128)S(1)} %get-tuple-element.29), channel_id=1, source_target_pairs={{0,1},{1,0},{2,3},{3,2},{4,5},{5,4},{6,7},{7,6},{8,9},{9,8},{10,11... | collective-permute-start | bytes 3538952 | tf_op jit(solution)/shard_map/ppermute | solution.py:356
  5.6 10.6 %collective-permute-start.7 = (bf16[4,128,128]{2,1,0:T(8,128)(2,1)S(1)}, bf16[4,128,128]{2,1,0:T(8,128)(2,1)S(1)}, u32[]{:S(2)}, u32[]{:S(2)}) collective-permute-start(bf16[4,128,128]{2,1,0:T(8,128)(2,1)S(1)} %bitcast.26), channel_id=1, source_target_pairs={{0,16},{4,20},{8,24},{12,28},{16,0},{20,4},{24,8},{28,12},{1,17},{... | collective-permute-start | bytes 393224 | tf_op jit(solution)/shard_map/ppermute | solution.py:356
  16.2 8.8 %collective-permute-start.8 = (bf16[8,128,128]{2,1,0:T(8,128)(2,1)S(1)}, bf16[8,128,128]{2,1,0:T(8,128)(2,1)S(1)}, u32[]{:S(2)}, u32[]{:S(2)}) collective-permute-start(bf16[8,128,128]{2,1,0:T(8,128)(2,1)S(1)} %pad_maximum_fusion.2.refs_5_), channel_id=1, source_target_pairs={{0,4},{4,0},{8,12},{12,8},{16,20},{20,16},{24,28},{28,24},{1,5},{5... | collective-permute-start | bytes 786440 | tf_op jit(solution)/shard_map/ppermute | solution.py:356
  17.8 25.7 %collective-permute-start.1 = (bf16[4,128,128]{2,1,0:T(8,128)(2,1)S(1)}, bf16[4,128,128]{2,1,0:T(8,128)(2,1)}, u32[]{:S(2)}, u32[]{:S(2)}) collective-permute-start(bf16[4,128,128]{2,1,0:T(8,128)(2,1)S(1)} %get-tuple-element.27.refs_2_), channel_id=1, source_target_pairs={{0,2},{1,3},{2,0},{3,1},{4,6},{5,7},{6,4},{7,5},{8,10},{9,11},{10,... | collective-permute-start | bytes 393224 | tf_op jit(solution)/shard_map/ppermute | solution.py:356
  19.3 9.4 %collective-permute-start.2 = (f32[64,256]{1,0:T(8,128)S(1)}, f32[64,256]{1,0:T(8,128)S(1)}, u32[]{:S(2)}, u32[]{:S(2)}) collective-permute-start(f32[64,256]{1,0:T(8,128)S(1)} %constant_dynamic-slice_fusion.2), channel_id=1, source_target_pairs={{0,4},{4,0},{8,12},{12,8},{16,20},{20,16},{24,28},{28,24},{1,5},{5... | collective-permute-start | bytes 196616 | tf_op jit(solution)/shard_map/ppermute | solution.py:356
  19.8 21.4 %collective-permute-start.9 = (bf16[8,128,128]{2,1,0:T(8,128)(2,1)S(1)}, bf16[8,128,128]{2,1,0:T(8,128)(2,1)}, u32[]{:S(2)}, u32[]{:S(2)}) collective-permute-start(bf16[8,128,128]{2,1,0:T(8,128)(2,1)S(1)} %pad_maximum_fusion.2.refs_5_), channel_id=1, source_target_pairs={{0,8},{4,12},{8,0},{12,4},{16,24},{20,28},{24,16},{28,20},{1,9},{5... | collective-permute-start | bytes 786440 | tf_op jit(solution)/shard_map/ppermute | solution.py:356
  25.0 16.8 %collective-permute-start.10 = (bf16[8,128,128]{2,1,0:T(8,128)(2,1)S(1)}, bf16[8,128,128]{2,1,0:T(8,128)(2,1)}, u32[]{:S(2)}, u32[]{:S(2)}) collective-permute-start(bf16[8,128,128]{2,1,0:T(8,128)(2,1)S(1)} %collective-permute-done.8.refs_6_), channel_id=1, source_target_pairs={{0,8},{4,12},{8,0},{12,4},{16,24},{20,28},{24,16},{28,20},{1,9},{5... | collective-permute-start | bytes 786440 | tf_op jit(solution)/shard_map/ppermute | solution.py:356
  27.1 14.8 %collective-permute-start.6 = (f32[576,256]{1,0:T(8,128)S(1)}, f32[576,256]{1,0:T(8,128)S(1)}, u32[]{:S(2)}, u32[]{:S(2)}) collective-permute-start(f32[576,256]{1,0:T(8,128)S(1)} %slice_add_fusion.1), channel_id=1, source_target_pairs={{0,2},{1,3},{2,0},{3,1},{4,6},{5,7},{6,4},{7,5},{8,10},{9,11},{10,... | collective-permute-start | bytes 1769480 | tf_op jit(solution)/shard_map/ppermute | solution.py:356
  33.9 6.5 %collective-permute-start.5 = (f32[64,256]{1,0:T(8,128)S(1)}, f32[64,256]{1,0:T(8,128)}, u32[]{:S(2)}, u32[]{:S(2)}) collective-permute-start(f32[64,256]{1,0:T(8,128)S(1)} %add.119), channel_id=1, source_target_pairs={{0,16},{4,20},{8,24},{12,28},{16,0},{20,4},{24,8},{28,12},{1,17},{... | collective-permute-start | bytes 196616 | tf_op jit(solution)/shard_map/ppermute | solution.py:356
  40.4 6.8 %collective-permute-start.11 = (bf16[8,128,128]{2,1,0:T(8,128)(2,1)S(1)}, bf16[8,128,128]{2,1,0:T(8,128)(2,1)S(1)}, u32[]{:S(2)}, u32[]{:S(2)}) collective-permute-start(bf16[8,128,128]{2,1,0:T(8,128)(2,1)S(1)} %pad_maximum_fusion.2.refs_5_), channel_id=1, source_target_pairs={{0,1},{1,0},{2,3},{3,2},{4,5},{5,4},{6,7},{7,6},{8,9},{9,8},{10,11... | collective-permute-start | bytes 786440 | tf_op jit(solution)/shard_map/ppermute | solution.py:356
  41.2 6.0 %collective-permute-start.12 = (bf16[8,128,128]{2,1,0:T(8,128)(2,1)S(1)}, bf16[8,128,128]{2,1,0:T(8,128)(2,1)S(1)}, u32[]{:S(2)}, u32[]{:S(2)}) collective-permute-start(bf16[8,128,128]{2,1,0:T(8,128)(2,1)S(1)} %collective-permute-done.8.refs_6_), channel_id=1, source_target_pairs={{0,1},{1,0},{2,3},{3,2},{4,5},{5,4},{6,7},{7,6},{8,9},{9,8},{10,11... | collective-permute-start | bytes 786440 | tf_op jit(solution)/shard_map/ppermute | solution.py:356
  41.8 5.4 %collective-permute-start.13 = (bf16[8,128,128]{2,1,0:T(8,128)(2,1)}, bf16[8,128,128]{2,1,0:T(8,128)(2,1)S(1)}, u32[]{:S(2)}, u32[]{:S(2)}) collective-permute-start(bf16[8,128,128]{2,1,0:T(8,128)(2,1)} %collective-permute-done.9.refs_7_), channel_id=1, source_target_pairs={{0,1},{1,0},{2,3},{3,2},{4,5},{5,4},{6,7},{7,6},{8,9},{9,8},{10,11... | collective-permute-start | bytes 786440 | tf_op jit(solution)/shard_map/ppermute | solution.py:356
  41.9 5.3 %collective-permute-start.14 = (bf16[8,128,128]{2,1,0:T(8,128)(2,1)}, bf16[8,128,128]{2,1,0:T(8,128)(2,1)S(1)}, u32[]{:S(2)}, u32[]{:S(2)}) collective-permute-start(bf16[8,128,128]{2,1,0:T(8,128)(2,1)} %collective-permute-done.10.refs_8_), channel_id=1, source_target_pairs={{0,1},{1,0},{2,3},{3,2},{4,5},{5,4},{6,7},{7,6},{8,9},{9,8},{10,11... | collective-permute-start | bytes 786440 | tf_op jit(solution)/shard_map/ppermute | solution.py:356
  58.7 4.6 %collective-permute-start.15 = (f32[1024,128]{1,0:T(8,128)S(1)}, f32[1024,128]{1,0:T(8,128)S(1)}, u32[]{:S(2)}, u32[]{:S(2)}) collective-permute-start(f32[1024,128]{1,0:T(8,128)S(1)} %get-tuple-element.40), channel_id=1, source_target_pairs={{0,1},{1,0},{2,3},{3,2},{4,5},{5,4},{6,7},{7,6},{8,9},{9,8},{10,11... | collective-permute-start | bytes 1572872 | tf_op jit(solution)/shard_map/ppermute | solution.py:356
  58.8 4.8 %collective-permute-start.18 = (f32[64,256]{1,0:T(8,128)S(1)}, f32[64,256]{1,0:T(8,128)S(1)}, u32[]{:S(2)}, u32[]{:S(2)}) collective-permute-start(f32[64,256]{1,0:T(8,128)S(1)} %fusion.3.refs_0_), channel_id=1, source_target_pairs={{0,1},{1,0},{2,3},{3,2},{4,5},{5,4},{6,7},{7,6},{8,9},{9,8},{10,11... | collective-permute-start | bytes 196616 | tf_op jit(solution)/shard_map/ppermute | solution.py:356
  63.3 9.7 %collective-permute-start.16 = (f32[512,128]{1,0:T(8,128)S(1)}, f32[512,128]{1,0:T(8,128)S(1)}, u32[]{:S(2)}, u32[]{:S(2)}) collective-permute-start(f32[512,128]{1,0:T(8,128)S(1)} %get-tuple-element.54), channel_id=1, source_target_pairs={{0,2},{1,3},{2,0},{3,1},{4,6},{5,7},{6,4},{7,5},{8,10},{9,11},{10,... | collective-permute-start | bytes 786440 | tf_op jit(solution)/shard_map/ppermute | solution.py:356
  75.4 5.0 %collective-permute-start.22 = (f32[64,256]{1,0:T(8,128)S(1)}, f32[64,256]{1,0:T(8,128)S(1)}, u32[]{:S(2)}, u32[]{:S(2)}) collective-permute-start(f32[64,256]{1,0:T(8,128)S(1)} %slice_add_fusion.4), channel_id=1, source_target_pairs={{0,2},{1,3},{2,0},{3,1},{4,6},{5,7},{6,4},{7,5},{8,10},{9,11},{10,... | collective-permute-start | bytes 196616 | tf_op jit(solution)/shard_map/ppermute | solution.py:356
  76.3 8.9 %collective-permute-start.20 = (bf16[512,256]{1,0:T(8,128)(2,1)S(1)}, bf16[512,256]{1,0:T(8,128)(2,1)S(1)}, u32[]{:S(2)}, u32[]{:S(2)}) collective-permute-start(bf16[512,256]{1,0:T(8,128)(2,1)S(1)} %get-tuple-element.44), channel_id=1, source_target_pairs={{0,2},{1,3},{2,0},{3,1},{4,6},{5,7},{6,4},{7,5},{8,10},{9,11},{10,... | collective-permute-start | bytes 786440 | tf_op jit(solution)/shard_map/ppermute | solution.py:356
  88.5 8.3 %collective-permute-start.25 = (f32[256,256]{0,1:T(8,128)S(1)}, f32[256,256]{0,1:T(8,128)S(1)}, u32[]{:S(2)}, u32[]{:S(2)}) collective-permute-start(f32[256,256]{0,1:T(8,128)S(1)} %dynamic-slice_bitcast_fusion), channel_id=1, source_target_pairs={{0,4},{4,0},{8,12},{12,8},{16,20},{20,16},{24,28},{28,24},{1,5},{5... | collective-permute-start | bytes 786440 | tf_op jit(solution)/shard_map/ppermute | solution.py:356
  93.0 6.2 %collective-permute-start.29 = (f32[64,256]{1,0:T(8,128)S(1)}, f32[64,256]{1,0:T(8,128)S(1)}, u32[]{:S(2)}, u32[]{:S(2)}) collective-permute-start(f32[64,256]{1,0:T(8,128)S(1)} %add.142), channel_id=1, source_target_pairs={{0,16},{4,20},{8,24},{12,28},{16,0},{20,4},{24,8},{28,12},{1,17},{... | collective-permute-start | bytes 196616 | tf_op jit(solution)/shard_map/ppermute | solution.py:356
  96.9 6.6 %collective-permute-start.26 = (f32[128,256]{0,1:T(8,128)S(1)}, f32[128,256]{0,1:T(8,128)S(1)}, u32[]{:S(2)}, u32[]{:S(2)}) collective-permute-start(f32[128,256]{0,1:T(8,128)S(1)} %constant_dynamic-slice_fusion), channel_id=1, source_target_pairs={{0,8},{4,12},{8,0},{12,4},{16,24},{20,28},{24,16},{28,20},{1,9},{5... | collective-permute-start | bytes 393224 | tf_op jit(solution)/shard_map/ppermute | solution.py:356
  100.3 6.7 %collective-permute-start.31 = (f32[64,256]{1,0:T(8,128)S(1)}, f32[64,256]{1,0:T(8,128)S(1)}, u32[]{:S(2)}, u32[]{:S(2)}) collective-permute-start(f32[64,256]{1,0:T(8,128)S(1)} %add.143.refs_0_), channel_id=1, source_target_pairs={{0,1},{1,0},{2,3},{3,2},{4,5},{5,4},{6,7},{7,6},{8,9},{9,8},{10,11... | collective-permute-start | bytes 196616 | tf_op jit(solution)/shard_map/ppermute | solution.py:356
  103.5 12.2 %collective-permute-start.27 = (f32[128,256]{0,1:T(8,128)S(1)}, f32[128,256]{0,1:T(8,128)S(1)}, u32[]{:S(2)}, u32[]{:S(2)}) collective-permute-start(f32[128,256]{0,1:T(8,128)S(1)} %dynamic-slice_add_fusion), channel_id=1, source_target_pairs={{0,16},{4,20},{8,24},{12,28},{16,0},{20,4},{24,8},{28,12},{1,17},{... | collective-permute-start | bytes 393224 | tf_op jit(solution)/shard_map/ppermute | solution.py:356
  120.5 5.0 %collective-permute-start.34 = (bf16[256,256]{1,0:T(8,128)(2,1)S(1)}, bf16[256,256]{1,0:T(8,128)(2,1)S(1)}, u32[]{:S(2)}, u32[]{:S(2)}) collective-permute-start(bf16[256,256]{1,0:T(8,128)(2,1)S(1)} %pad_maximum_fusion.4), channel_id=1, source_target_pairs={{0,4},{4,0},{8,12},{12,8},{16,20},{20,16},{24,28},{28,24},{1,5},{5... | collective-permute-start | bytes 393224 | tf_op jit(solution)/shard_map/ppermute | solution.py:356
  (18 other events, 80.1 us)

commit v2 on v1

--- a/solution.py
+++ b/solution.py
@@ -272,43 +272,33 @@
     data[3] = jnp.where(alive, val[...].astype(F32), 0.0).astype(BF16)
 
 
-def tiles_kernel(n_tables, unit, meta_hbm, meta_par_hbm, own_hbm, par_hbm, ctx_hbm, *rest):
+def tiles_kernel(n_tables, unit, meta_ref, meta_par_ref, own_ref, par_ref, ctx_ref, *rest):
     tables = rest[:n_tables]
-    outs = rest[n_tables:-8]
-    table_ref, raw_ref, ctx_ref, data_ref, acc_ref, meta_own, meta_par, sems = rest[-8:]
-    total, width = own_hbm.shape[1:]
+    outs = rest[n_tables:-6]
+    table_ref, data_ref, acc_ref, meta_own, meta_par, sems = rest[-6:]
+    total, width = own_ref.shape[1:]
     copies = [
-        pltpu.make_async_copy(own_hbm, raw_ref.at[0], sems.at[0]),
-        pltpu.make_async_copy(par_hbm, raw_ref.at[1], sems.at[1]),
-        pltpu.make_async_copy(meta_hbm, meta_own, sems.at[2]),
-        pltpu.make_async_copy(meta_par_hbm, meta_par, sems.at[3]),
-        pltpu.make_async_copy(ctx_hbm, ctx_ref, sems.at[4]),
+        pltpu.make_async_copy(meta_ref, meta_own, sems.at[0]),
+        pltpu.make_async_copy(meta_par_ref, meta_par, sems.at[1]),
     ]
-    start = 0
-    for i, source in enumerate(tables):
-        count = source.shape[0]
-        copies.append(
-            pltpu.make_async_copy(source, table_ref.at[pl.ds(start, count)], sems.at[5 + i])
-        )
-        start += count
     for copy in copies:
         copy.start()
+    start = 0
+    for source in tables:
+        table_ref[start : start + source.shape[0]] = source[...]
+        start += source.shape[0]
     acc_ref[...] = jnp.zeros_like(acc_ref)
-    copies[0].wait()
-    data_ref[:, :total, :] = raw_ref[0].astype(F32)
-    copies[1].wait()
-    data_ref[:, total:, :] = raw_ref[1].astype(F32)
+    data_ref[:, :total, :] = own_ref[...].astype(F32)
+    data_ref[:, total:, :] = par_ref[...].astype(F32)
     big = lax.broadcasted_iota(jnp.int32, (SLAB, width), 0).astype(F32).astype(BF16)
     wide = lax.broadcasted_iota(jnp.int32, (CB, width), 0).astype(F32).astype(BF16)
     small = lax.broadcasted_iota(jnp.int32, (UB, width), 0).astype(F32).astype(BF16)
     one, zero = jnp.ones((), BF16), jnp.zeros((), BF16)
     flip = kernel_ids(unit)[1]
-    copies[2].wait()
-    copies[3].wait()
+    for copy in copies:
+        copy.wait()
     own_groups = (meta_own[4, 0] + UNROLL - 1) // UNROLL
     groups = own_groups + (meta_par[4, 0] + UNROLL - 1) // UNROLL
-    for copy in copies[4:]:
-        copy.wait()
 
     def group(g, _):
         is_own = g < own_groups
@@ -424,9 +414,7 @@
 
     def place(slab, ids):
         owner, inner = slab // held, slab % held
-        far = owner ^ ids[0]
-        position = sum((far // d % 2) * (1 << n) for n, d in enumerate(steps))
-        return ((inner // part ^ ids[2]) * size + position) * part + inner % part
+        return ((inner // part ^ ids[2]) * size + (owner ^ ids[0])) * part + inner % part
 
     return piece, steps, place
 
@@ -492,8 +480,11 @@
     )
 
     user_steps = halves(lax.axis_size("users"))[::-1]
+    first = after(piece, data)
+    pieces = {0: piece}
     if steps:
-        came = swap(after(piece, data), "users", steps[0])
+        for d in steps:
+            pieces[d] = swap(first, "users", d)
     rank_rows = rank_width // items_size
     levels = dense_parts(after(profile, (data, piece)), feature_factors, items_size)
     item_part = take_rows(gram(after(item_factors, levels[-1])), index * rank_rows, rank_rows)
@@ -501,26 +492,31 @@
     meta_other = swap(meta, "items", top)
     data_other = swap(data, "items", top)
     if steps:
-        tables = [jnp.concatenate([piece, after(came, item_part)], 0)]
-        tables += [swap(tables[0], "users", d) for d in steps[1:2]]
-        early = [swap(tables[0], "users", d) for d in steps[2:3]]
+        for e in sorted(range(1, lax.axis_size("users")), key=lambda e: bin(e).count("1")):
+            hops = [d for d in steps if e & d]
+            if len(hops) % 2:
+                hops = hops[:-2] + hops[:-3:-1]
+            if len(hops) > 1:
+                pieces[e] = swap(pieces[e ^ hops[-1]], "users", hops[-1])
+        tables = [pieces[e] for e in range(lax.axis_size("users"))]
     else:
         full = lax.all_gather(piece, "users", tiled=True)
-        tables, early = [full.reshape(-1, SLAB, cols).transpose(0, 2, 1)], []
+        tables = [full.reshape(-1, SLAB, cols).transpose(0, 2, 1)]
     levels = scatter_levels(levels, order[:-1])
     dense_other = swap(levels[1], "items", top)
     late = after(context_factors, levels[1])
     contexts = lax.dynamic_slice_in_dim(late, high * cols, cols, 1)
     contexts = contexts.reshape(-1, CB, cols).transpose(0, 2, 1)
     context_part = take_rows(gram(late), index * rank_rows, rank_rows)
-    if early:
-        tables = tables + early + [swap(tables[1], "users", steps[2])]
     item_part = item_part + after(item_other, levels[1])
     for distance in user_steps[1:]:
         item_part = item_part + swap(item_part, "users", distance)
     if steps:
         for distance in halves(top)[::-1]:
-            tables = tables + [swap(x, "items", distance) for x in tables]
+            tables = tables + [
+                swap(after(x, contexts) if n == len(tables) // 2 else x, "items", distance)
+                for n, x in enumerate(tables)
+            ]
     dense = levels[0] + after(dense_other, item_part)
     diagonal = (
         index * rank_rows + lax.broadcasted_iota(jnp.int32, item_part.shape, 0)
@@ -535,19 +531,17 @@
         lambda *refs: tiles_kernel(len(tables), user_rows, *refs),
         name="tiles",
         out_shape=[pltpu.VMEM((n, cols), F32) for n in sizes],
-        in_specs=[ANY] * (5 + len(tables)),
+        in_specs=[VM] * (5 + len(tables)),
         cost_estimate=cost(15),
         compiler_params=pltpu.CompilerParams(vmem_limit_bytes=VMEM_GRANT),
         out_specs=[VM] * len(sizes),
         scratch_shapes=[
             pltpu.VMEM((sum(t.shape[0] for t in tables), cols, SLAB), BF16),
-            pltpu.VMEM((2,) + data.shape, BF16),
-            pltpu.VMEM(contexts.shape, BF16),
             pltpu.VMEM((4, 2 * tile_total, width), F32),
             pltpu.VMEM((slab_users, cols), F32),
             pltpu.SMEM(meta.shape, jnp.int32),
             pltpu.SMEM(meta.shape, jnp.int32),
-            pltpu.SemaphoreType.DMA((5 + len(tables),)),
+            pltpu.SemaphoreType.DMA((2,)),
         ],
     )(*here(meta, meta_other, data, data_other, contexts, *tables))
     mine, near = scatter_levels(levels, order[:-1])

time: 127 us -> 124 us (0.976)
  starting transfers between devices: 34.2 us -> 45.5 us
  waiting for transfers between devices: 47.2 us -> 36.5 us
  other arithmetic: 6.28 us -> 3.73 us
    ppermute x35 -> x42, starting transfers between devices: 34.2 us -> 45.5 us  [swap(): return lax.ppermute(x, axis, [(i, i ^ distance) for i in range(size)])]
    ppermute x35 -> x42, waiting for transfers between devices: 47.2 us -> 36.5 us  [swap(): return lax.ppermute(x, axis, [(i, i ^ distance) for i in range(size)])]
  transfers between devices with their start and end apart: 35 -> 42, of which waited for: 18 -> 18; matrix products, arithmetic and copies ran while one was open for 5% -> 3% of each run, Pallas kernels for 14% -> 14%
where the time goes in v2:
time: 124 us; the launch traced here: 123 us
  starting transfers between devices  45.5 us (37%)
  waiting for transfers between devices  36.5 us (29%)
  Pallas kernels  30.9 us (25%)
  other arithmetic  3.73 us (3%)
  matrix products  2.98 us (2%)
  local copies, waits for them, and re-layouts  2.09 us (2%)
  between operations  1.72 us (1%)
    ppermute x42, starting transfers between devices, swap(): return lax.ppermute(x, axis, [(i, i ^ distance) for i in range(size)])  45.5 us
    ppermute x42, waiting for transfers between devices, swap(): return lax.ppermute(x, axis, [(i, i ^ distance) for i in range(size)])  36.5 us
    pallas_call x2, Pallas kernels, inverse(): pl.pallas_call(lambda *refs: inverse_kernel(ridge, *refs), out_shape=pltp...  17.2 us
    pallas_call x1, Pallas kernels, local(): pl.pallas_call(lambda *refs: tiles_kernel(len(tables), user_rows, *refs),...  10.8 us
  transfers between devices with their start and end apart: 42, of which 18 were waited for; matrix products, arithmetic and copies ran while one was open for 3% of the time, Pallas kernels for 14%

profile of v2, /device:TPU:0, one launch (start us, length us, event | category | flops | bytes accessed | tf_op | source)
XLA Modules:
  0.0 123.5 jit_solution(4517538555467138470)
XLA Ops:
  9.3 2.9 %collective-permute-start.6 = (f32[576,256]{1,0:T(8,128)S(1)}, f32[576,256]{1,0:T(8,128)S(1)}, u32[]{:S(2)}, u32[]{:S(2)}) collective-permute-start(f32[576,256]{1,0:T(8,128)S(1)} %slice_add_fusion.1), channel_id=1, source_target_pairs={{0,2},{1,3},{2,0},{3,1},{4,6},{5,7},{6,4},{7,5},{8,10},{9,11},{10,... | collective-permute-start | bytes 1769480 | tf_op jit(solution)/shard_map/ppermute | solution.py:346
  14.3 2.6 %collective-permute-start.10 = (bf16[4,128,128]{2,1,0:T(8,128)(2,1)S(1)}, bf16[4,128,128]{2,1,0:T(8,128)(2,1)S(1)}, u32[]{:S(2)}, u32[]{:S(2)}) collective-permute-start(bf16[4,128,128]{2,1,0:T(8,128)(2,1)S(1)} %bitcast.24), channel_id=1, source_target_pairs={{0,16},{4,20},{8,24},{12,28},{16,0},{20,4},{24,8},{28,12},{1,17},{... | collective-permute-start | bytes 393224 | tf_op jit(solution)/shard_map/ppermute | solution.py:346
  20.1 3.3 %collective-permute-done.4 = f32[64,256]{1,0:T(8,128)S(1)} collective-permute-done((f32[64,256]{1,0:T(8,128)S(1)}, f32[64,256]{1,0:T(8,128)S(1)}, u32[]{:S(2)}, u32[]{:S(2)}) %collective-permute-start.4) | collective-permute-done | bytes 65568 | tf_op jit(solution)/shard_map/ppermute | solution.py:346
  23.4 2.0 %collective-permute-start.5 = (f32[64,256]{1,0:T(8,128)S(1)}, f32[64,256]{1,0:T(8,128)S(1)}, u32[]{:S(2)}, u32[]{:S(2)}) collective-permute-start(f32[64,256]{1,0:T(8,128)S(1)} %add.119), channel_id=1, source_target_pairs={{0,16},{4,20},{8,24},{12,28},{16,0},{20,4},{24,8},{28,12},{1,17},{... | collective-permute-start | bytes 196616 | tf_op jit(solution)/shard_map/ppermute | solution.py:346
  25.9 2.9 %collective-permute-done.refs_1_ = s32[8,128]{1,0:T(8,128)S(1)} collective-permute-done((s32[8,128]{1,0:T(8,128)S(1)}, s32[8,128]{1,0:T(8,128)S(1)}, u32[]{:S(2)}, u32[]{:S(2)}) %collective-permute-start) | collective-permute-done | bytes 4128 | tf_op jit(solution)/shard_map/ppermute | solution.py:346
  28.8 1.8 %collective-permute-start.8 = (bf16[4,128,128]{2,1,0:T(8,128)(2,1)S(1)}, bf16[4,128,128]{2,1,0:T(8,128)(2,1)S(1)}, u32[]{:S(2)}, u32[]{:S(2)}) collective-permute-start(bf16[4,128,128]{2,1,0:T(8,128)(2,1)S(1)} %bitcast.26), channel_id=1, source_target_pairs={{0,8},{4,12},{8,0},{12,4},{16,24},{20,28},{24,16},{28,20},{1,9},{5... | collective-permute-start | bytes 393224 | tf_op jit(solution)/shard_map/ppermute | solution.py:346
  31.3 1.8 %collective-permute-start.11 = (bf16[4,128,128]{2,1,0:T(8,128)(2,1)S(1)}, bf16[4,128,128]{2,1,0:T(8,128)(2,1)S(1)}, u32[]{:S(2)}, u32[]{:S(2)}) collective-permute-start(bf16[4,128,128]{2,1,0:T(8,128)(2,1)S(1)} %collective-permute-done.10.refs_9_), channel_id=1, source_target_pairs={{0,4},{4,0},{8,12},{12,8},{16,20},{20,16},{24,28},{28,24},{1,5},{5... | collective-permute-start | bytes 393224 | tf_op jit(solution)/shard_map/ppermute | solution.py:346
  35.2 1.9 %collective-permute-done.12.refs_11_ = bf16[4,128,128]{2,1,0:T(8,128)(2,1)S(1)} collective-permute-done((bf16[4,128,128]{2,1,0:T(8,128)(2,1)S(1)}, bf16[4,128,128]{2,1,0:T(8,128)(2,1)S(1)}, u32[]{:S(2)}, u32[]{:S(2)}) %collective-permute-start.12) | collective-permute-done | bytes 131104 | tf_op jit(solution)/shard_map/ppermute | solution.py:346
  43.6 10.8 %tiles.1 = (f32[512,128]{1,0:T(8,128)S(1)}, f32[512,128]{1,0:T(8,128)S(1)}, f32[1024,128]{1,0:T(8,128)S(1)}) custom-call(s32[8,128]{1,0:T(8,128)S(1)} %get-tuple-element.26.refs_0_, s32[8,128]{1,0:T(8,128)S(1)} %collective-permute-done.refs_1_, bf16[4,128,128]{2,1,0:T(8,128)(2,1)S(1)} %get-tuple-element.27.refs_2_, ...), custom_call_target="tpu_custom_call" | custom-call | flops 15000000512 | tf_op jit(solution)/shard_map/tiles/pallas_call | solution.py:530
  56.4 2.6 %collective-permute-done.24.refs_1_ = f32[64,256]{1,0:T(8,128)S(1)} collective-permute-done((f32[64,256]{1,0:T(8,128)S(1)}, f32[64,256]{1,0:T(8,128)S(1)}, u32[]{:S(2)}, u32[]{:S(2)}) %collective-permute-start.24) | collective-permute-done | bytes 65568 | tf_op jit(solution)/shard_map/ppermute | solution.py:346
  60.8 8.5 %shard_map.142.refs_3_ = f32[256,256]{1,0:T(8,128)S(1)} custom-call(f32[64,256]{1,0:T(8,128)S(1)} %fusion.3.refs_0_, f32[64,256]{1,0:T(8,128)S(1)} %collective-permute-done.24.refs_1_, f32[64,256]{1,0:T(8,128)S(1)} %collective-permute-done.25.refs_2_, f32[64,256]{1,0:T(8,128)S(1)} %collective-permute-done.26.refs_3_), custom_call_target="tpu_custom_call" | custom-call | flops 11000000512 | tf_op jit(solution)/shard_map/pallas_call | solution.py:136
  73.7 2.9 %collective-permute-done.29 = f32[64,256]{1,0:T(8,128)S(1)} collective-permute-done((f32[64,256]{1,0:T(8,128)S(1)}, f32[64,256]{1,0:T(8,128)S(1)}, u32[]{:S(2)}, u32[]{:S(2)}) %collective-permute-start.29) | collective-permute-done | bytes 65568 | tf_op jit(solution)/shard_map/ppermute | solution.py:346
  78.3 2.6 %collective-permute-done.30 = f32[64,256]{1,0:T(8,128)S(1)} collective-permute-done((f32[64,256]{1,0:T(8,128)S(1)}, f32[64,256]{1,0:T(8,128)S(1)}, u32[]{:S(2)}, u32[]{:S(2)}) %collective-permute-start.30) | collective-permute-done | bytes 65568 | tf_op jit(solution)/shard_map/ppermute | solution.py:346
  81.8 1.9 %collective-permute-done.31 = bf16[1024,256]{1,0:T(8,128)(2,1)S(1)} collective-permute-done((bf16[1024,256]{1,0:T(8,128)(2,1)S(1)}, bf16[1024,256]{1,0:T(8,128)(2,1)S(1)}, u32[]{:S(2)}, u32[]{:S(2)}) %collective-permute-start.31) | collective-permute-done | bytes 524320 | tf_op jit(solution)/shard_map/ppermute | solution.py:346
  86.5 2.4 %collective-permute-start.35 = (f32[64,256]{1,0:T(8,128)S(1)}, f32[64,256]{1,0:T(8,128)S(1)}, u32[]{:S(2)}, u32[]{:S(2)}) collective-permute-start(f32[64,256]{1,0:T(8,128)S(1)} %add.132), channel_id=1, source_target_pairs={{0,8},{4,12},{8,0},{12,4},{16,24},{20,28},{24,16},{28,20},{1,9},{5... | collective-permute-start | bytes 196616 | tf_op jit(solution)/shard_map/ppermute | solution.py:346
  88.9 2.2 %collective-permute-done.35 = f32[64,256]{1,0:T(8,128)S(1)} collective-permute-done((f32[64,256]{1,0:T(8,128)S(1)}, f32[64,256]{1,0:T(8,128)S(1)}, u32[]{:S(2)}, u32[]{:S(2)}) %collective-permute-start.35) | collective-permute-done | bytes 65568 | tf_op jit(solution)/shard_map/ppermute | solution.py:346
  91.2 2.7 %collective-permute-start.36 = (f32[64,256]{1,0:T(8,128)S(1)}, f32[64,256]{1,0:T(8,128)S(1)}, u32[]{:S(2)}, u32[]{:S(2)}) collective-permute-start(f32[64,256]{1,0:T(8,128)S(1)} %add.142), channel_id=1, source_target_pairs={{0,16},{4,20},{8,24},{12,28},{16,0},{20,4},{24,8},{28,12},{1,17},{... | collective-permute-start | bytes 196616 | tf_op jit(solution)/shard_map/ppermute | solution.py:346
  94.0 2.1 %collective-permute-start.33 = (f32[128,256]{0,1:T(8,128)S(1)}, f32[128,256]{0,1:T(8,128)S(1)}, u32[]{:S(2)}, u32[]{:S(2)}) collective-permute-start(f32[128,256]{0,1:T(8,128)S(1)} %constant_dynamic-slice_fusion), channel_id=1, source_target_pairs={{0,8},{4,12},{8,0},{12,4},{16,24},{20,28},{24,16},{28,20},{1,9},{5... | collective-permute-start | bytes 393224 | tf_op jit(solution)/shard_map/ppermute | solution.py:346
  97.8 3.2 %collective-permute-done.37.refs_1_ = f32[64,256]{1,0:T(8,128)S(1)} collective-permute-done((f32[64,256]{1,0:T(8,128)S(1)}, f32[64,256]{1,0:T(8,128)S(1)}, u32[]{:S(2)}, u32[]{:S(2)}) %collective-permute-start.37) | collective-permute-done | bytes 65568 | tf_op jit(solution)/shard_map/ppermute | solution.py:346
  101.1 2.9 %collective-permute-start.34 = (f32[128,256]{0,1:T(8,128)S(1)}, f32[128,256]{0,1:T(8,128)S(1)}, u32[]{:S(2)}, u32[]{:S(2)}) collective-permute-start(f32[128,256]{0,1:T(8,128)S(1)} %dynamic-slice_add_fusion), channel_id=1, source_target_pairs={{0,16},{4,20},{8,24},{12,28},{16,0},{20,4},{24,8},{28,12},{1,17},{... | collective-permute-start | bytes 393224 | tf_op jit(solution)/shard_map/ppermute | solution.py:346
  104.0 8.7 %shard_map.144 = f32[256,256]{1,0:T(8,128)S(1)} custom-call(f32[64,256]{1,0:T(8,128)S(1)} %add.143.refs_0_, f32[64,256]{1,0:T(8,128)S(1)} %collective-permute-done.37.refs_1_, f32[64,256]{1,0:T(8,128)S(1)} %collective-permute-done.38.refs_2_, f32[64,256]{1,0:T(8,128)S(1)} %collective-permute-done.39.refs_3_), custom_call_target="tpu_custom_call" | custom-call | flops 11000000512 | tf_op jit(solution)/shard_map/pallas_call | solution.py:136
  113.1 2.0 %collective-permute-start.40 = (bf16[128,256]{1,0:T(8,128)(2,1)S(1)}, bf16[128,256]{1,0:T(8,128)(2,1)S(1)}, u32[]{:S(2)}, u32[]{:S(2)}) collective-permute-start(bf16[128,256]{1,0:T(8,128)(2,1)S(1)} %convolution_convert_fusion), channel_id=1, source_target_pairs={{0,8},{4,12},{8,0},{12,4},{16,24},{20,28},{24,16},{28,20},{1,9},{5... | collective-permute-start | bytes 196616 | tf_op jit(solution)/shard_map/ppermute | solution.py:346
  115.1 2.5 %collective-permute-done.40 = bf16[128,256]{1,0:T(8,128)(2,1)S(1)} collective-permute-done((bf16[128,256]{1,0:T(8,128)(2,1)S(1)}, bf16[128,256]{1,0:T(8,128)(2,1)S(1)}, u32[]{:S(2)}, u32[]{:S(2)}) %collective-permute-start.40) | collective-permute-done | bytes 65568 | tf_op jit(solution)/shard_map/ppermute | solution.py:346
  118.1 4.6 %collective-permute-done.41 = bf16[256,256]{1,0:T(8,128)(2,1)S(1)} collective-permute-done((bf16[256,256]{1,0:T(8,128)(2,1)S(1)}, bf16[256,256]{1,0:T(8,128)(2,1)S(1)}, u32[]{:S(2)}, u32[]{:S(2)}) %collective-permute-start.41) | collective-permute-done | bytes 131104 | tf_op jit(solution)/shard_map/ppermute | solution.py:346
  (110 shorter events, 39.7 us)
Async XLA Ops:
  9.3 21.3 %collective-permute-start.6 = (f32[576,256]{1,0:T(8,128)S(1)}, f32[576,256]{1,0:T(8,128)S(1)}, u32[]{:S(2)}, u32[]{:S(2)}) collective-permute-start(f32[576,256]{1,0:T(8,128)S(1)} %slice_add_fusion.1), channel_id=1, source_target_pairs={{0,2},{1,3},{2,0},{3,1},{4,6},{5,7},{6,4},{7,5},{8,10},{9,11},{10,... | collective-permute-start | bytes 1769480 | tf_op jit(solution)/shard_map/ppermute | solution.py:346
  12.3 6.1 %collective-permute-start.2 = (f32[64,256]{1,0:T(8,128)S(1)}, f32[64,256]{1,0:T(8,128)S(1)}, u32[]{:S(2)}, u32[]{:S(2)}) collective-permute-start(f32[64,256]{1,0:T(8,128)S(1)} %constant_dynamic-slice_fusion.2), channel_id=1, source_target_pairs={{0,4},{4,0},{8,12},{12,8},{16,20},{20,16},{24,28},{28,24},{1,5},{5... | collective-permute-start | bytes 196616 | tf_op jit(solution)/shard_map/ppermute | solution.py:346
  13.8 17.5 %collective-permute-start.1 = (bf16[4,128,128]{2,1,0:T(8,128)(2,1)S(1)}, bf16[4,128,128]{2,1,0:T(8,128)(2,1)S(1)}, u32[]{:S(2)}, u32[]{:S(2)}) collective-permute-start(bf16[4,128,128]{2,1,0:T(8,128)(2,1)S(1)} %get-tuple-element.27.refs_2_), channel_id=1, source_target_pairs={{0,2},{1,3},{2,0},{3,1},{4,6},{5,7},{6,4},{7,5},{8,10},{9,11},{10,... | collective-permute-start | bytes 393224 | tf_op jit(solution)/shard_map/ppermute | solution.py:346
  14.3 11.4 %collective-permute-start.10 = (bf16[4,128,128]{2,1,0:T(8,128)(2,1)S(1)}, bf16[4,128,128]{2,1,0:T(8,128)(2,1)S(1)}, u32[]{:S(2)}, u32[]{:S(2)}) collective-permute-start(bf16[4,128,128]{2,1,0:T(8,128)(2,1)S(1)} %bitcast.24), channel_id=1, source_target_pairs={{0,16},{4,20},{8,24},{12,28},{16,0},{20,4},{24,8},{28,12},{1,17},{... | collective-permute-start | bytes 393224 | tf_op jit(solution)/shard_map/ppermute | solution.py:346
  16.9 11.9 %collective-permute-start = (s32[8,128]{1,0:T(8,128)S(1)}, s32[8,128]{1,0:T(8,128)S(1)}, u32[]{:S(2)}, u32[]{:S(2)}) collective-permute-start(s32[8,128]{1,0:T(8,128)S(1)} %get-tuple-element.26.refs_0_), channel_id=1, source_target_pairs={{0,2},{1,3},{2,0},{3,1},{4,6},{5,7},{6,4},{7,5},{8,10},{9,11},{10,... | collective-permute-start | bytes 12296 | tf_op jit(solution)/shard_map/ppermute | solution.py:346
  18.4 5.0 %collective-permute-start.4 = (f32[64,256]{1,0:T(8,128)S(1)}, f32[64,256]{1,0:T(8,128)S(1)}, u32[]{:S(2)}, u32[]{:S(2)}) collective-permute-start(f32[64,256]{1,0:T(8,128)S(1)} %fusion.14), channel_id=1, source_target_pairs={{0,8},{4,12},{8,0},{12,4},{16,24},{20,28},{24,16},{28,20},{1,9},{5... | collective-permute-start | bytes 196616 | tf_op jit(solution)/shard_map/ppermute | solution.py:346
  23.4 7.2 %collective-permute-start.5 = (f32[64,256]{1,0:T(8,128)S(1)}, f32[64,256]{1,0:T(8,128)S(1)}, u32[]{:S(2)}, u32[]{:S(2)}) collective-permute-start(f32[64,256]{1,0:T(8,128)S(1)} %add.119), channel_id=1, source_target_pairs={{0,16},{4,20},{8,24},{12,28},{16,0},{20,4},{24,8},{28,12},{1,17},{... | collective-permute-start | bytes 196616 | tf_op jit(solution)/shard_map/ppermute | solution.py:346
  25.7 7.4 %collective-permute-start.7 = (bf16[4,128,128]{2,1,0:T(8,128)(2,1)S(1)}, bf16[4,128,128]{2,1,0:T(8,128)(2,1)S(1)}, u32[]{:S(2)}, u32[]{:S(2)}) collective-permute-start(bf16[4,128,128]{2,1,0:T(8,128)(2,1)S(1)} %bitcast.25), channel_id=1, source_target_pairs={{0,4},{4,0},{8,12},{12,8},{16,20},{20,16},{24,28},{28,24},{1,5},{5... | collective-permute-start | bytes 393224 | tf_op jit(solution)/shard_map/ppermute | solution.py:346
  28.8 5.8 %collective-permute-start.8 = (bf16[4,128,128]{2,1,0:T(8,128)(2,1)S(1)}, bf16[4,128,128]{2,1,0:T(8,128)(2,1)S(1)}, u32[]{:S(2)}, u32[]{:S(2)}) collective-permute-start(bf16[4,128,128]{2,1,0:T(8,128)(2,1)S(1)} %bitcast.26), channel_id=1, source_target_pairs={{0,8},{4,12},{8,0},{12,4},{16,24},{20,28},{24,16},{28,20},{1,9},{5... | collective-permute-start | bytes 393224 | tf_op jit(solution)/shard_map/ppermute | solution.py:346
  30.6 6.4 %collective-permute-start.12 = (bf16[4,128,128]{2,1,0:T(8,128)(2,1)S(1)}, bf16[4,128,128]{2,1,0:T(8,128)(2,1)S(1)}, u32[]{:S(2)}, u32[]{:S(2)}) collective-permute-start(bf16[4,128,128]{2,1,0:T(8,128)(2,1)S(1)} %collective-permute-done.10.refs_9_), channel_id=1, source_target_pairs={{0,8},{4,12},{8,0},{12,4},{16,24},{20,28},{24,16},{28,20},{1,9},{5... | collective-permute-start | bytes 393224 | tf_op jit(solution)/shard_map/ppermute | solution.py:346
  31.3 8.8 %collective-permute-start.11 = (bf16[4,128,128]{2,1,0:T(8,128)(2,1)S(1)}, bf16[4,128,128]{2,1,0:T(8,128)(2,1)S(1)}, u32[]{:S(2)}, u32[]{:S(2)}) collective-permute-start(bf16[4,128,128]{2,1,0:T(8,128)(2,1)S(1)} %collective-permute-done.10.refs_9_), channel_id=1, source_target_pairs={{0,4},{4,0},{8,12},{12,8},{16,20},{20,16},{24,28},{28,24},{1,5},{5... | collective-permute-start | bytes 393224 | tf_op jit(solution)/shard_map/ppermute | solution.py:346
  33.1 6.9 %collective-permute-start.9 = (bf16[4,128,128]{2,1,0:T(8,128)(2,1)S(1)}, bf16[4,128,128]{2,1,0:T(8,128)(2,1)S(1)}, u32[]{:S(2)}, u32[]{:S(2)}) collective-permute-start(bf16[4,128,128]{2,1,0:T(8,128)(2,1)S(1)} %collective-permute-done.7.refs_6_), channel_id=1, source_target_pairs={{0,8},{4,12},{8,0},{12,4},{16,24},{20,28},{24,16},{28,20},{1,9},{5... | collective-permute-start | bytes 393224 | tf_op jit(solution)/shard_map/ppermute | solution.py:346
  34.7 5.9 %collective-permute-start.15 = (bf16[4,128,128]{2,1,0:T(8,128)(2,1)S(1)}, bf16[4,128,128]{2,1,0:T(8,128)(2,1)S(1)}, u32[]{:S(2)}, u32[]{:S(2)}) collective-permute-start(bf16[4,128,128]{2,1,0:T(8,128)(2,1)S(1)} %collective-permute-done.7.refs_6_), channel_id=1, source_target_pairs={{0,1},{1,0},{2,3},{3,2},{4,5},{5,4},{6,7},{7,6},{8,9},{9,8},{10,11... | collective-permute-start | bytes 393224 | tf_op jit(solution)/shard_map/ppermute | solution.py:346
  34.7 7.4 %collective-permute-start.16 = (bf16[4,128,128]{2,1,0:T(8,128)(2,1)S(1)}, bf16[4,128,128]{2,1,0:T(8,128)(2,1)S(1)}, u32[]{:S(2)}, u32[]{:S(2)}) collective-permute-start(bf16[4,128,128]{2,1,0:T(8,128)(2,1)S(1)} %collective-permute-done.8.refs_7_), channel_id=1, source_target_pairs={{0,1},{1,0},{2,3},{3,2},{4,5},{5,4},{6,7},{7,6},{8,9},{9,8},{10,11... | collective-permute-start | bytes 393224 | tf_op jit(solution)/shard_map/ppermute | solution.py:346
  37.1 5.0 %collective-permute-start.13 = (bf16[4,128,128]{2,1,0:T(8,128)(2,1)S(1)}, bf16[4,128,128]{2,1,0:T(8,128)(2,1)S(1)}, u32[]{:S(2)}, u32[]{:S(2)}) collective-permute-start(bf16[4,128,128]{2,1,0:T(8,128)(2,1)S(1)} %collective-permute-done.12.refs_11_), channel_id=1, source_target_pairs={{0,4},{4,0},{8,12},{12,8},{16,20},{20,16},{24,28},{28,24},{1,5},{5... | collective-permute-start | bytes 393224 | tf_op jit(solution)/shard_map/ppermute | solution.py:346
  59.1 10.2 %collective-permute-start.23 = (f32[512,128]{1,0:T(8,128)S(1)}, f32[512,128]{1,0:T(8,128)S(1)}, u32[]{:S(2)}, u32[]{:S(2)}) collective-permute-start(f32[512,128]{1,0:T(8,128)S(1)} %get-tuple-element.54), channel_id=1, source_target_pairs={{0,2},{1,3},{2,0},{3,1},{4,6},{5,7},{6,4},{7,5},{8,10},{9,11},{10,... | collective-permute-start | bytes 786440 | tf_op jit(solution)/shard_map/ppermute | solution.py:346
  71.6 5.0 %collective-permute-start.29 = (f32[64,256]{1,0:T(8,128)S(1)}, f32[64,256]{1,0:T(8,128)S(1)}, u32[]{:S(2)}, u32[]{:S(2)}) collective-permute-start(f32[64,256]{1,0:T(8,128)S(1)} %slice_add_fusion.4), channel_id=1, source_target_pairs={{0,2},{1,3},{2,0},{3,1},{4,6},{5,7},{6,4},{7,5},{8,10},{9,11},{10,... | collective-permute-start | bytes 196616 | tf_op jit(solution)/shard_map/ppermute | solution.py:346
  72.8 8.8 %collective-permute-start.27 = (bf16[512,256]{1,0:T(8,128)(2,1)S(1)}, bf16[512,256]{1,0:T(8,128)(2,1)S(1)}, u32[]{:S(2)}, u32[]{:S(2)}) collective-permute-start(bf16[512,256]{1,0:T(8,128)(2,1)S(1)} %get-tuple-element.44), channel_id=1, source_target_pairs={{0,2},{1,3},{2,0},{3,1},{4,6},{5,7},{6,4},{7,5},{8,10},{9,11},{10,... | collective-permute-start | bytes 786440 | tf_op jit(solution)/shard_map/ppermute | solution.py:346
  84.9 9.0 %collective-permute-start.32 = (f32[256,256]{0,1:T(8,128)S(1)}, f32[256,256]{0,1:T(8,128)S(1)}, u32[]{:S(2)}, u32[]{:S(2)}) collective-permute-start(f32[256,256]{0,1:T(8,128)S(1)} %dynamic-slice_bitcast_fusion), channel_id=1, source_target_pairs={{0,4},{4,0},{8,12},{12,8},{16,20},{20,16},{24,28},{28,24},{1,5},{5... | collective-permute-start | bytes 786440 | tf_op jit(solution)/shard_map/ppermute | solution.py:346
  91.2 5.5 %collective-permute-start.36 = (f32[64,256]{1,0:T(8,128)S(1)}, f32[64,256]{1,0:T(8,128)S(1)}, u32[]{:S(2)}, u32[]{:S(2)}) collective-permute-start(f32[64,256]{1,0:T(8,128)S(1)} %add.142), channel_id=1, source_target_pairs={{0,16},{4,20},{8,24},{12,28},{16,0},{20,4},{24,8},{28,12},{1,17},{... | collective-permute-start | bytes 196616 | tf_op jit(solution)/shard_map/ppermute | solution.py:346
  94.0 7.1 %collective-permute-start.33 = (f32[128,256]{0,1:T(8,128)S(1)}, f32[128,256]{0,1:T(8,128)S(1)}, u32[]{:S(2)}, u32[]{:S(2)}) collective-permute-start(f32[128,256]{0,1:T(8,128)S(1)} %constant_dynamic-slice_fusion), channel_id=1, source_target_pairs={{0,8},{4,12},{8,0},{12,4},{16,24},{20,28},{24,16},{28,20},{1,9},{5... | collective-permute-start | bytes 393224 | tf_op jit(solution)/shard_map/ppermute | solution.py:346
  97.8 6.2 %collective-permute-start.38 = (f32[64,256]{1,0:T(8,128)S(1)}, f32[64,256]{1,0:T(8,128)S(1)}, u32[]{:S(2)}, u32[]{:S(2)}) collective-permute-start(f32[64,256]{1,0:T(8,128)S(1)} %add.143.refs_0_), channel_id=1, source_target_pairs={{0,1},{1,0},{2,3},{3,2},{4,5},{5,4},{6,7},{7,6},{8,9},{9,8},{10,11... | collective-permute-start | bytes 196616 | tf_op jit(solution)/shard_map/ppermute | solution.py:346
  101.1 11.6 %collective-permute-start.34 = (f32[128,256]{0,1:T(8,128)S(1)}, f32[128,256]{0,1:T(8,128)S(1)}, u32[]{:S(2)}, u32[]{:S(2)}) collective-permute-start(f32[128,256]{0,1:T(8,128)S(1)} %dynamic-slice_add_fusion), channel_id=1, source_target_pairs={{0,16},{4,20},{8,24},{12,28},{16,0},{20,4},{24,8},{28,12},{1,17},{... | collective-permute-start | bytes 393224 | tf_op jit(solution)/shard_map/ppermute | solution.py:346
  117.6 5.1 %collective-permute-start.41 = (bf16[256,256]{1,0:T(8,128)(2,1)S(1)}, bf16[256,256]{1,0:T(8,128)(2,1)S(1)}, u32[]{:S(2)}, u32[]{:S(2)}) collective-permute-start(bf16[256,256]{1,0:T(8,128)(2,1)S(1)} %pad_maximum_fusion.3), channel_id=1, source_target_pairs={{0,4},{4,0},{8,12},{12,8},{16,20},{20,16},{24,28},{28,24},{1,5},{5... | collective-permute-start | bytes 393224 | tf_op jit(solution)/shard_map/ppermute | solution.py:346
  (23 other events, 88.0 us)
